TPU v7x, 128 devices: a whole 4x4x4 slice. The times are simulated.
128 devices in a mesh: seg: 16 (over y, z_lo, core), tile: 8 (over x, z_hi).
Axes of the slice: x: 4, y: 4, z: 4 (z_hi: 2, z_lo: 2; z = z_hi * 2 + z_lo), core: 2. Of those that a mesh axis runs over, the one named last changes fastest.
Arguments:
- path_field: float32 [128, 128, 64, 128], P('seg', 'tile'), may hold values from -1.2 to 1.2
- counts: int32 [16], replicated, may hold values from 0 to 16, as said below
- offsets: int32 [128], replicated, may hold values from 0 to 6
- weights: float32 [128], replicated, may hold values from 0 to 1
Outputs:
- new_path: float32 [128, 128, 64, 128], P('seg', 'tile')
Inputs may be any that keep to these rules, and one draw needn't show every extreme that they name: counts sum to 128; for every segment s the running sum of counts before s differs from s * 8 by at most 4; the first segment supplies 8 + 8 // 2 new images, and a segment of 16 new images occurs in every draw.
All inputs are finite; a program needn't handle non-finite values.
Results may differ from a plain program's by a relative error of at most 0.00002.
Values sent between devices are 32-bit elements; how exact they have to be, the bound alone decides.
No kernel may reach another device: no remote copies, remote signals or barrier semaphores. Data moves between devices by JAX's collectives and lax.ppermute only.
A program may use at most 128 MiB of HBM per device.

v0:
```python
import functools

import jax
import jax.numpy as jnp
from jax import lax
from jax.experimental import pallas as pl
from jax.experimental.pallas import tpu as pltpu
from jax.sharding import PartitionSpec as P


KAPPA_COEF = 1.0
TIME_STEP = 0.1
DESCENT_RATE = 0.01


AXES = ("seg", "tile")
ANY = pl.BlockSpec(memory_space=pl.ANY)
VMEM = pl.BlockSpec(memory_space=pltpu.VMEM)
SMEM = pl.BlockSpec(memory_space=pltpu.SMEM)


def routes(segs, tiles, ds_of, dt):
    pairs = []
    for s in range(segs):
        for t in range(tiles):
            to_s, to_t = s + ds_of(s), t + dt
            if 0 <= to_s < segs and 0 <= to_t < tiles:
                pairs.append((s * tiles + t, to_s * tiles + to_t))
    return pairs


def outer(s):
    return 1 if s % 2 else -1


def inner(s):
    return -1 if s % 2 else 1


def neighbour_sum(ref, j, x, c):
    total = ref[j, x + 1] + ref[j, x - 1]
    for axis in (0, 1):
        total = total + (pltpu.roll(c, 1, axis) + pltpu.roll(c, c.shape[axis] - 1, axis))
    return total


def each_plane(images, planes, body):
    def over_images(j, carry):
        def over_planes(x, inner_carry):
            body(j, x)
            return inner_carry

        return lax.fori_loop(planes[0], planes[1], over_planes, carry, unroll=planes[1] - planes[0])

    lax.fori_loop(images[0], images[1], over_images, 0)


def residual_stage(p, r, images, planes):
    def body(j, x):
        c = p[j, x]
        linear = 6.0 * KAPPA_COEF - 1.0 - 1.0 / TIME_STEP
        total = neighbour_sum(p, j, x, c)
        if KAPPA_COEF != 1.0:
            total = KAPPA_COEF * total
        r[j, x] = p[j + 1, x] * (1.0 / TIME_STEP) - total + c * (c * c + linear)

    each_plane(images, planes, body)


def update_stage(p, r, images, planes, first_id, last_id):
    def body(j, x):
        c = p[j, x]
        rc = r[j, x]
        linear = 1.0 + TIME_STEP * (1.0 - 6.0 * KAPPA_COEF)
        pull = rc * (linear - (3.0 * TIME_STEP) * (c * c)) - r[j - 1, x]
        down = (TIME_STEP * KAPPA_COEF) * neighbour_sum(r, j, x, rc) + pull
        image_id = first_id + j
        rate = jnp.where((image_id > 0) & (image_id < last_id), DESCENT_RATE, 0.0)
        p[j, x] = c + rate * down

    each_plane(images, planes, body)


def clear(ref, images, planes):
    def body(j, x):
        ref[j, x] = jnp.zeros(ref.shape[2:], ref.dtype)

    each_plane(images, planes, body)


def descend(p, r, images, s, segs, outside):
    n = p.shape[1]
    first_id, last_id = s * images - 2, segs * images - 1
    for step in range(2):
        lo, hi = 2 * step + 1, n - 2 * step - 1
        residual_stage(p, r, (step, images + 3 - step), (lo, hi))

        @pl.when(s == 0)
        def _():
            clear(r, (step, 2), (lo, hi))

        @pl.when(s == segs - 1)
        def _():
            clear(r, (images + 1, images + 3 - step), (lo, hi))

        for cond, planes in outside:

            @pl.when(cond)
            def _(planes=planes):
                clear(r, (step, images + 3 - step), planes)

        update_stage(
            p, r, (step + 1, images + 3 - step), (lo + 1, hi - 1), first_id, last_id
        )
        if step == 0:
            for cond, planes in outside:

                @pl.when(cond)
                def _(planes=planes):
                    clear(p, (1, images + 3), planes)


def mix(weights, offsets, k, p, base, x):
    w = weights[k]
    q = offsets[k] + base
    return w * p[q, x] + (1.0 - w) * p[q + 1, x]


def run_copies(copies):
    for c in copies:
        c.start()
    for c in copies:
        c.wait()


def outer_base(s, images):
    core = lax.rem(s, 2)
    half = images // 2
    k = jnp.where(core == 0, s * images - half, (s + 1) * images)
    return jnp.clip(k, 0, None)


def inner_base(s, images):
    core = lax.rem(s, 2)
    half = images // 2
    return jnp.where(core == 0, (s + 1) * images, s * images - half)


def inside_kernel(
    segs, place, offsets, weights, path, from_outer, from_inner, p2, slots, p, r, sems
):
    images, n = path.shape[0], path.shape[1]
    s = place[0]
    core = lax.rem(s, 2)
    run_copies(
        [
            pltpu.make_async_copy(path, p.at[pl.ds(2, images)], sems.at[0]),
            pltpu.make_async_copy(
                from_outer, p.at[pl.ds(jnp.where(core == 0, 0, images + 2), 2)], sems.at[1]
            ),
            pltpu.make_async_copy(
                from_inner, p.at[pl.ds(jnp.where(core == 0, images + 2, 0), 2)], sems.at[2]
            ),
        ]
    )
    descend(p, r, images, s, segs, ())
    half = images // 2
    total = segs * images
    k0 = outer_base(s, images)

    def to_slots(i, x):
        k = jnp.minimum(k0 + i, total - 1)
        slots[i, x] = mix(weights, offsets, k, p, 2, x + 4)

    each_plane((0, half), (0, n - 8), to_slots)

    def to_p2(j, x):
        p2[j, x] = p[j + 2, x + 4]

    each_plane((0, images), (0, n - 8), to_p2)


def edge_kernel(
    segs,
    tiles,
    low,
    place,
    offsets,
    weights,
    path,
    from_outer,
    from_inner,
    beyond,
    corner_outer,
    corner_inner,
    p2,
    slots,
    p,
    r,
    sems,
):
    images, n = path.shape[0], path.shape[1]
    s, t = place[0], place[1]
    core = lax.rem(s, 2)
    outer_near = jnp.where(core == 0, 1, images + 2)
    outer_far = jnp.where(core == 0, 0, images + 3)
    inner_near = jnp.where(core == 0, images + 2, 1)
    inner_far = jnp.where(core == 0, images + 3, 0)
    outer_row = jnp.where(core == 0, 0, images + 2)
    inner_row = jnp.where(core == 0, images + 2, 0)
    own, at = (pl.ds(0, 8), pl.ds(4, 8)) if low else (pl.ds(n - 8, 8), pl.ds(0, 8))
    three, two = (pl.ds(1, 3), pl.ds(2, 2)) if low else (pl.ds(8, 3), pl.ds(8, 2))
    plan = [
        (path.at[:, own], p.at[pl.ds(2, images), at]),
        (from_outer.at[:, own], p.at[pl.ds(outer_row, 2), at]),
        (from_inner.at[:, own], p.at[pl.ds(inner_row, 2), at]),
        (beyond, p.at[pl.ds(2, images), pl.ds(0 if low else 8, 4)]),
        (corner_outer.at[pl.ds(0, 3)], p.at[outer_near, three]),
        (corner_outer.at[pl.ds(3, 2)], p.at[outer_far, two]),
        (corner_inner.at[pl.ds(0, 3)], p.at[inner_near, three]),
        (corner_inner.at[pl.ds(3, 2)], p.at[inner_far, two]),
    ]
    run_copies([pltpu.make_async_copy(a, b, sems.at[i]) for i, (a, b) in enumerate(plan)])
    half = images // 2
    total = segs * images
    k0 = outer_base(s, images)
    outside = (t == 0, (1, 4)) if low else (t == tiles - 1, (8, 11))
    descend(p, r, images, s, segs, (outside,))

    def to_slots(i, x):
        k = jnp.minimum(k0 + i, total - 1)
        slots[i, x] = mix(weights, offsets, k, p, 2, x + 4)

    each_plane((0, half), (0, 4), to_slots)

    def to_p2(j, x):
        p2[j, x] = p[j + 2, x + 4]

    each_plane((0, images), (0, 4), to_p2)


def corner_kernel(low, first_if_zero, place, src, out, sems):
    images, width = src.shape[0], src.shape[1]
    at_first = (lax.rem(place[0], 2) == 0) == first_if_zero
    near = jnp.where(at_first, 0, images - 1)
    far = jnp.where(at_first, 1, images - 2)
    three, two = (pl.ds(0, 3), pl.ds(0, 2)) if low else (pl.ds(width - 3, 3), pl.ds(width - 2, 2))
    run_copies(
        [
            pltpu.make_async_copy(src.at[near, three], out.at[pl.ds(0, 3)], sems.at[0]),
            pltpu.make_async_copy(src.at[far, two], out.at[pl.ds(3, 2)], sems.at[1]),
        ]
    )


def pair_kernel(first_if_zero, place, path, out, sems):
    images = path.shape[0]
    at_first = (lax.rem(place[0], 2) == 0) == first_if_zero
    first = jnp.where(at_first, 0, images - 2)
    run_copies([pltpu.make_async_copy(path.at[pl.ds(first, 2)], out, sems.at[0])])


def plane_parts(n):
    return ((0, 4, 0), (4, n - 4, 1), (n - 4, n, 2))


def inner_slots_kernel(place, offsets, weights, low, inside, high, slots):
    images, n = inside.shape[0], slots.shape[1]
    half = images // 2
    k0 = inner_base(place[0], images)
    for lo, hi, which in plane_parts(n):
        p = (low, inside, high)[which]

        def body(i, x):
            slots[i, x + lo] = mix(weights, offsets, k0 + i, p, 0, x)

        each_plane((0, half), (0, hi - lo), body)


def own_kernel(place, offsets, weights, low, inside, high, out):
    images, n = out.shape[0], out.shape[1]
    k0 = place[0] * images
    for lo, hi, which in plane_parts(n):
        p = (low, inside, high)[which]

        def body(i, x):
            out[i, x + lo] = mix(weights, offsets, k0 + i, p, 0, x)

        each_plane((0, images), (0, hi - lo), body)


def source_step(counts, k, s, segs):
    end = jnp.int32(0)
    source = jnp.int32(0)
    for i in range(segs):
        end = end + counts[i]
        source = source + jnp.where(end <= k, 1, 0)
    return source - s


def place_kernel(segs, place, counts, low, inside, high, inner_part, own, out, sems):
    del own
    images, n = out.shape[0], out.shape[1]
    half = images // 2
    s = place[0]
    core = lax.rem(s, 2)

    def copies(i, slot, from_outer):
        for lo, hi, which in plane_parts(n):
            if from_outer:
                src = (low, inside, high)[which].at[slot]
            else:
                src = inner_part.at[slot, pl.ds(lo, hi - lo)]
            yield pltpu.make_async_copy(src, out.at[i, pl.ds(lo, hi - lo)], sems.at[i, which])

    for start in (True, False):
        for i in range(images):
            step = source_step(counts, s * images + i, s, segs)
            slot = i % half
            foreign = (step < 0) if i < half else (step > 0)
            outer_core = 0 if i < half else 1

            for from_outer in (True, False):

                @pl.when(foreign & ((core == outer_core) == from_outer))
                def _(i=i, slot=slot, from_outer=from_outer):
                    for c in copies(i, slot, from_outer):
                        if start:
                            c.start()
                        else:
                            c.wait()


def field(*shape):
    return jax.ShapeDtypeStruct(shape, jnp.float32)


def cost(planes, arrays):
    return pl.CostEstimate(
        flops=planes * 8192 * 60, bytes_accessed=arrays * 2**20, transcendentals=0
    )


def params(mib):
    return pltpu.CompilerParams(vmem_limit_bytes=mib * 2**20)


def step(path_field, counts, offsets, weights):
    images, n, gy, gz = path_field.shape
    segs, tiles = lax.axis_size("seg"), lax.axis_size("tile")
    s, t = lax.axis_index("seg"), lax.axis_index("tile")
    half = images // 2
    place = jnp.stack([s, t]).astype(jnp.int32)

    def send(block, ds_of, dt):
        return lax.ppermute(block, AXES, routes(segs, tiles, ds_of, dt))

    def stay(_):
        return 0

    def call(kernel, *args, **settings):
        return pl.pallas_call(kernel, **settings)(*args)

    def corner(array, low, first_if_zero):
        return call(
            functools.partial(corner_kernel, low, first_if_zero),
            place,
            array,
            out_shape=field(5, gy, gz),
            in_specs=[SMEM, ANY],
            out_specs=VMEM,
            scratch_shapes=[pltpu.SemaphoreType.DMA((2,))],
            compiler_params=params(1),
            cost_estimate=cost(0, 1),
        )

    def pair(first_if_zero):
        return call(
            functools.partial(pair_kernel, first_if_zero),
            place,
            path_field,
            out_shape=field(2, n, gy, gz),
            in_specs=[SMEM, ANY],
            out_specs=VMEM,
            scratch_shapes=[pltpu.SemaphoreType.DMA((1,))],
            compiler_params=params(2),
            cost_estimate=cost(0, 2),
        )

    from_outer = send(pair(True), outer, 0)
    from_inner = send(pair(False), inner, 0)
    below = send(path_field[:, n - 4 :], stay, 1)
    above = send(path_field[:, :4], stay, -1)
    corner_below = send(corner(path_field, False, True), outer, 1)
    corner_above = send(corner(path_field, True, True), outer, -1)

    p2_inside, slots_inside = call(
        functools.partial(inside_kernel, segs),
        place,
        offsets,
        weights,
        path_field,
        from_outer,
        from_inner,
        out_shape=(field(images, n - 8, gy, gz), field(half, n - 8, gy, gz)),
        in_specs=[SMEM, SMEM, SMEM, ANY, ANY, ANY],
        out_specs=(VMEM, VMEM),
        scratch_shapes=[
            pltpu.VMEM((images + 4, n, gy, gz), jnp.float32),
            pltpu.VMEM((images + 3, n, gy, gz), jnp.float32),
            pltpu.SemaphoreType.DMA((3,)),
        ],
        compiler_params=params(18),
        cost_estimate=cost(44 * 10, 8),
    )
    got_inside = send(slots_inside, outer, 0)

    def edge(low, beyond, corner_outer):
        corner_inner = send(corner(beyond, not low, False), inner, 0)
        return call(
            functools.partial(edge_kernel, segs, tiles, low),
            place,
            offsets,
            weights,
            path_field,
            from_outer,
            from_inner,
            beyond,
            corner_outer,
            corner_inner,
            out_shape=(field(images, 4, gy, gz), field(half, 4, gy, gz)),
            in_specs=[SMEM, SMEM, SMEM] + [ANY] * 6,
            out_specs=(VMEM, VMEM),
            scratch_shapes=[
                pltpu.VMEM((images + 4, 12, gy, gz), jnp.float32),
                pltpu.VMEM((images + 3, 12, gy, gz), jnp.float32),
                pltpu.SemaphoreType.DMA((8,)),
            ],
            compiler_params=params(14),
            cost_estimate=cost(28 * 10, 6),
        )

    p2_low, slots_low = edge(True, below, corner_below)
    got_low = send(slots_low, outer, 0)
    p2_high, slots_high = edge(False, above, corner_above)
    got_high = send(slots_high, outer, 0)

    slots_inner = call(
        inner_slots_kernel,
        place,
        offsets,
        weights,
        p2_low,
        p2_inside,
        p2_high,
        out_shape=field(half, n, gy, gz),
        in_specs=[SMEM, SMEM, SMEM, VMEM, VMEM, VMEM],
        out_specs=VMEM,
        compiler_params=params(8),
        cost_estimate=cost(16, 6),
    )
    got_inner = send(slots_inner, inner, 0)
    own = call(
        own_kernel,
        place,
        offsets,
        weights,
        p2_low,
        p2_inside,
        p2_high,
        out_shape=field(images, n, gy, gz),
        in_specs=[SMEM, SMEM, SMEM, VMEM, VMEM, VMEM],
        out_specs=VMEM,
        compiler_params=params(10),
        cost_estimate=cost(32, 8),
    )
    return call(
        functools.partial(place_kernel, segs),
        place,
        counts,
        got_low,
        got_inside,
        got_high,
        got_inner,
        own,
        out_shape=field(images, n, gy, gz),
        in_specs=[SMEM, SMEM, VMEM, VMEM, VMEM, VMEM, ANY],
        out_specs=ANY,
        scratch_shapes=[pltpu.SemaphoreType.DMA((images, 3))],
        input_output_aliases={6: 0},
        compiler_params=params(6),
        cost_estimate=cost(2, 4),
    )


def solution(mesh):
    return jax.shard_map(
        step,
        mesh=mesh,
        in_specs=(P("seg", "tile", None, None), P(), P(), P()),
        out_specs=P("seg", "tile", None, None),
        check_vma=False,
    )
```

profile of v0, /device:TPU:48, one launch (start us, length us, event | category | flops | bytes accessed | tf_op | source)
XLA Modules:
  0.0 164.1 jit_solution(8180766372713595591)
XLA Ops:
  0.0 2.7 %fusion = (f32[8,4,64,128]{3,2,1,0:T(8,128)}, f32[8,4,64,128]{3,2,1,0:T(8,128)S(1)}) fusion(f32[8,16,64,128]{3,2,1,0:T(8,128)} %path.9), kind=kLoop, calls=%fused_computation.1 | loop fusion | bytes 4194304 | tf_op jit(solution)/shard_map/slice | solution.py:393
  2.7 1.3 collective-permute-start.7
  4.0 6.1 %collective-permute-start.2 = (f32[8,4,64,128]{3,2,1,0:T(8,128)S(1)}, f32[8,4,64,128]{3,2,1,0:T(8,128)S(1)}, u32[]{:S(2)}, u32[]{:S(2)}) collective-permute-start(f32[8,4,64,128]{3,2,1,0:T(8,128)S(1)} %get-tuple-element.18), channel_id=1, source_target_pairs={{0,1},{1,2},{2,3},{3,4},{4,5},{5,6},{6,7},{8,9},{9,10},{10,11},{11... | collective-permute-start | bytes 3145736 | tf_op jit(solution)/shard_map/ppermute | solution.py:356
  10.1 0.1 pad_add_fusion.place
  10.2 0.0 copy-start
  10.2 2.2 %copy-done = f32[8,16,64,128]{3,2,1,0:T(8,128)S(1)} copy-done((f32[8,16,64,128]{3,2,1,0:T(8,128)S(1)}, f32[8,16,64,128]{3,2,1,0:T(8,128)}, u32[]{:S(2)}) %copy-start) | copy-done | bytes 4194328
  12.4 0.0 copy-start.1
  12.4 0.6 shard_map.46
  13.0 2.1 %collective-permute-start = (f32[2,16,64,128]{3,2,1,0:T(8,128)S(1)}, f32[2,16,64,128]{3,2,1,0:T(8,128)S(1)}, u32[]{:S(2)}, u32[]{:S(2)}) collective-permute-start(f32[2,16,64,128]{3,2,1,0:T(8,128)S(1)} %shard_map.46), channel_id=1, source_target_pairs={{8,16},{9,17},{10,18},{11,19},{12,20},{13,21},{14,22},{15,23},{16,... | collective-permute-start | bytes 3145736 | tf_op jit(solution)/shard_map/ppermute | solution.py:356
  15.1 0.6 shard_map.47
  15.7 1.4 collective-permute-start.1
  17.1 0.0 copy-done.1
  17.1 0.8 shard_map.52
  17.9 0.0 copy-start.2
  17.9 0.0 copy-start.3
  17.9 1.3 collective-permute-start.8
  19.2 24.5 %collective-permute-done.7.src.beyond = f32[8,4,64,128]{3,2,1,0:T(8,128)S(1)} collective-permute-done((f32[8,4,64,128]{3,2,1,0:T(8,128)}, f32[8,4,64,128]{3,2,1,0:T(8,128)S(1)}, u32[]{:S(2)}, u32[]{:S(2)}) %collective-permute-start.7) | collective-permute-done | bytes 1048608 | tf_op jit(solution)/shard_map/ppermute | solution.py:356
  43.7 0.8 shard_map.53
  44.5 0.1 collective-permute-start.9
  44.6 0.8 shard_map.48
  45.4 21.1 %collective-permute-done.2.src.beyond = f32[8,4,64,128]{3,2,1,0:T(8,128)S(1)} collective-permute-done((f32[8,4,64,128]{3,2,1,0:T(8,128)S(1)}, f32[8,4,64,128]{3,2,1,0:T(8,128)S(1)}, u32[]{:S(2)}, u32[]{:S(2)}) %collective-permute-start.2) | collective-permute-done | bytes 1048608 | tf_op jit(solution)/shard_map/ppermute | solution.py:356
  66.5 6.2 %collective-permute-start.3 = (f32[5,64,128]{2,1,0:T(8,128)S(1)}, f32[5,64,128]{2,1,0:T(8,128)S(1)}, u32[]{:S(2)}, u32[]{:S(2)}) collective-permute-start(f32[5,64,128]{2,1,0:T(8,128)S(1)} %shard_map.48), channel_id=1, source_target_pairs={{8,17},{9,18},{10,19},{11,20},{12,21},{13,22},{14,23},{16,9},{17,1... | collective-permute-start | bytes 491528 | tf_op jit(solution)/shard_map/ppermute | solution.py:356
  72.7 0.8 shard_map.49
  73.5 7.4 %collective-permute-done.from_outer = f32[2,16,64,128]{3,2,1,0:T(8,128)S(1)} collective-permute-done((f32[2,16,64,128]{3,2,1,0:T(8,128)S(1)}, f32[2,16,64,128]{3,2,1,0:T(8,128)S(1)}, u32[]{:S(2)}, u32[]{:S(2)}) %collective-permute-start) | collective-permute-done | bytes 1048608 | tf_op jit(solution)/shard_map/ppermute | solution.py:356
  81.0 0.0 collective-permute-start.4
  81.0 0.0 collective-permute-done.1.from_inner
  81.0 0.0 copy-done.2
  81.0 0.0 copy-done.3
  81.0 11.4 %shard_map.51 = (f32[8,8,64,128]{3,2,1,0:T(8,128)S(1)}, f32[4,8,64,128]{3,2,1,0:T(8,128)S(1)}) custom-call(s32[2]{0:T(128)S(1)} %pad_add_fusion.place, s32[128]{0:T(128)S(1)} %copy-done.2, f32[128]{0:T(128)S(1)} %copy-done.3, f32[8,16,64,128]{3,2,1,0:T(8,128)S(1)} %copy-done.1, f32[2,16,64,128]{3,2,1,0:T(8,128)S(1)} %collective-permute-done.from_outer, ...), custom_call_target="tpu_custom_call" | custom-call | flops 216268800 | bytes 8388608 | tf_op jit(solution)/shard_map/pallas_call | solution.py:362
  92.4 0.0 collective-permute-done.8.corner_outer
  92.4 0.0 collective-permute-done.9.corner_inner
  92.4 9.0 %shard_map.54 = (f32[8,4,64,128]{3,2,1,0:T(8,128)S(1)}, f32[4,4,64,128]{3,2,1,0:T(8,128)S(1)}) custom-call(s32[2]{0:T(128)S(1)} %pad_add_fusion.place, s32[128]{0:T(128)S(1)} %copy-done.2, f32[128]{0:T(128)S(1)} %copy-done.3, f32[8,16,64,128]{3,2,1,0:T(8,128)S(1)} %copy-done.1, f32[2,16,64,128]{3,2,1,0:T(8,128)S(1)} %collective-permute-done.from_outer, ...), custom_call_target="tpu_custom_call" | custom-call | flops 137625600 | bytes 6291456 | tf_op jit(solution)/shard_map/pallas_call | solution.py:362
  101.4 0.0 collective-permute-done.3.corner_outer
  101.4 0.0 collective-permute-done.4.corner_inner
  101.4 9.2 %shard_map.50 = (f32[8,4,64,128]{3,2,1,0:T(8,128)S(1)}, f32[4,4,64,128]{3,2,1,0:T(8,128)S(1)}) custom-call(s32[2]{0:T(128)S(1)} %pad_add_fusion.place, s32[128]{0:T(128)S(1)} %copy-done.2, f32[128]{0:T(128)S(1)} %copy-done.3, f32[8,16,64,128]{3,2,1,0:T(8,128)S(1)} %copy-done.1, f32[2,16,64,128]{3,2,1,0:T(8,128)S(1)} %collective-permute-done.from_outer, ...), custom_call_target="tpu_custom_call" | custom-call | flops 137625600 | bytes 6291456 | tf_op jit(solution)/shard_map/pallas_call | solution.py:362
  110.6 0.9 shard_map.55
  111.5 0.6 collective-permute-start.11
  112.1 1.9 %collective-permute-start.6 = (f32[4,8,64,128]{3,2,1,0:T(8,128)S(1)}, f32[4,8,64,128]{3,2,1,0:T(8,128)S(1)}, u32[]{:S(2)}, u32[]{:S(2)}) collective-permute-start(f32[4,8,64,128]{3,2,1,0:T(8,128)S(1)} %get-tuple-element.12), channel_id=1, source_target_pairs={{8,16},{9,17},{10,18},{11,19},{12,20},{13,21},{14,22},{15,23},{16,... | collective-permute-start | bytes 3145736 | tf_op jit(solution)/shard_map/ppermute | solution.py:356
  114.0 3.6 %collective-permute-start.10 = (f32[4,4,64,128]{3,2,1,0:T(8,128)S(1)}, f32[4,4,64,128]{3,2,1,0:T(8,128)S(1)}, u32[]{:S(2)}, u32[]{:S(2)}) collective-permute-start(f32[4,4,64,128]{3,2,1,0:T(8,128)S(1)} %get-tuple-element.13), channel_id=1, source_target_pairs={{8,16},{9,17},{10,18},{11,19},{12,20},{13,21},{14,22},{15,23},{16,... | collective-permute-start | bytes 1572872 | tf_op jit(solution)/shard_map/ppermute | solution.py:356
  117.6 0.0 copy-start.4
  117.7 1.9 %collective-permute-start.5 = (f32[4,4,64,128]{3,2,1,0:T(8,128)S(1)}, f32[4,4,64,128]{3,2,1,0:T(8,128)S(1)}, u32[]{:S(2)}, u32[]{:S(2)}) collective-permute-start(f32[4,4,64,128]{3,2,1,0:T(8,128)S(1)} %get-tuple-element.11), channel_id=1, source_target_pairs={{8,16},{9,17},{10,18},{11,19},{12,20},{13,21},{14,22},{15,23},{16,... | collective-permute-start | bytes 1572872 | tf_op jit(solution)/shard_map/ppermute | solution.py:356
  119.6 3.2 %shard_map.56.own = f32[8,16,64,128]{3,2,1,0:T(8,128)} custom-call(s32[2]{0:T(128)S(1)} %pad_add_fusion.place, s32[128]{0:T(128)S(1)} %copy-done.2, f32[128]{0:T(128)S(1)} %copy-done.3, f32[8,4,64,128]{3,2,1,0:T(8,128)S(1)} %get-tuple-element.14.low, f32[8,8,64,128]{3,2,1,0:T(8,128)S(1)} %get-tuple-element.15.inside, ...), custom_call_target="tpu_custom_call" | custom-call | flops 15728640 | bytes 8388608 | tf_op jit(solution)/shard_map/pallas_call | solution.py:362
  122.8 33.5 %collective-permute-done.10.high = f32[4,4,64,128]{3,2,1,0:T(8,128)S(1)} collective-permute-done((f32[4,4,64,128]{3,2,1,0:T(8,128)S(1)}, f32[4,4,64,128]{3,2,1,0:T(8,128)S(1)}, u32[]{:S(2)}, u32[]{:S(2)}) %collective-permute-start.10) | collective-permute-done | bytes 524320 | tf_op jit(solution)/shard_map/ppermute | solution.py:356
  156.3 5.6 %collective-permute-done.5.low = f32[4,4,64,128]{3,2,1,0:T(8,128)S(1)} collective-permute-done((f32[4,4,64,128]{3,2,1,0:T(8,128)S(1)}, f32[4,4,64,128]{3,2,1,0:T(8,128)S(1)}, u32[]{:S(2)}, u32[]{:S(2)}) %collective-permute-start.5) | collective-permute-done | bytes 524320 | tf_op jit(solution)/shard_map/ppermute | solution.py:356
  161.9 0.0 collective-permute-done.6.inside
  161.9 0.0 collective-permute-done.11.inner_part
  161.9 0.0 copy-done.4
  161.9 2.2 %shard_map.57 = f32[8,16,64,128]{3,2,1,0:T(8,128)} custom-call(s32[2]{0:T(128)S(1)} %pad_add_fusion.place, s32[16]{0:T(128)S(1)} %copy-done.4, f32[4,4,64,128]{3,2,1,0:T(8,128)S(1)} %collective-permute-done.5.low, f32[4,8,64,128]{3,2,1,0:T(8,128)S(1)} %collective-permute-done.6.inside, ...), custom_call_target="tpu_custom_call", output_to_operand_aliasing={{}: (6, {})} | custom-call | flops 983040 | bytes 4194304 | tf_op jit(solution)/shard_map/pallas_call | solution.py:362
Async XLA Ops:
  2.7 41.0 %collective-permute-start.7 = (f32[8,4,64,128]{3,2,1,0:T(8,128)}, f32[8,4,64,128]{3,2,1,0:T(8,128)S(1)}, u32[]{:S(2)}, u32[]{:S(2)}) collective-permute-start(f32[8,4,64,128]{3,2,1,0:T(8,128)} %get-tuple-element.17), channel_id=1, source_target_pairs={{1,0},{2,1},{3,2},{4,3},{5,4},{6,5},{7,6},{9,8},{10,9},{11,10},{12... | collective-permute-start | bytes 3145736 | tf_op jit(solution)/shard_map/ppermute | solution.py:356
  4.0 62.5 %collective-permute-start.2 = (f32[8,4,64,128]{3,2,1,0:T(8,128)S(1)}, f32[8,4,64,128]{3,2,1,0:T(8,128)S(1)}, u32[]{:S(2)}, u32[]{:S(2)}) collective-permute-start(f32[8,4,64,128]{3,2,1,0:T(8,128)S(1)} %get-tuple-element.18), channel_id=1, source_target_pairs={{0,1},{1,2},{2,3},{3,4},{4,5},{5,6},{6,7},{8,9},{9,10},{10,11},{11... | collective-permute-start | bytes 3145736 | tf_op jit(solution)/shard_map/ppermute | solution.py:356
  10.2 2.2 %copy-start = (f32[8,16,64,128]{3,2,1,0:T(8,128)S(1)}, f32[8,16,64,128]{3,2,1,0:T(8,128)}, u32[]{:S(2)}) copy-start(f32[8,16,64,128]{3,2,1,0:T(8,128)} %path.9) | copy-start | bytes 12582916
  12.4 4.7 %copy-start.1 = (f32[8,16,64,128]{3,2,1,0:T(8,128)S(1)}, f32[8,16,64,128]{3,2,1,0:T(8,128)}, u32[]{:S(2)}) copy-start(f32[8,16,64,128]{3,2,1,0:T(8,128)} %path.9) | copy-start | bytes 12582916
  13.0 67.9 %collective-permute-start = (f32[2,16,64,128]{3,2,1,0:T(8,128)S(1)}, f32[2,16,64,128]{3,2,1,0:T(8,128)S(1)}, u32[]{:S(2)}, u32[]{:S(2)}) collective-permute-start(f32[2,16,64,128]{3,2,1,0:T(8,128)S(1)} %shard_map.46), channel_id=1, source_target_pairs={{8,16},{9,17},{10,18},{11,19},{12,20},{13,21},{14,22},{15,23},{16,... | collective-permute-start | bytes 3145736 | tf_op jit(solution)/shard_map/ppermute | solution.py:356
  15.7 65.2 %collective-permute-start.1 = (f32[2,16,64,128]{3,2,1,0:T(8,128)S(1)}, f32[2,16,64,128]{3,2,1,0:T(8,128)S(1)}, u32[]{:S(2)}, u32[]{:S(2)}) collective-permute-start(f32[2,16,64,128]{3,2,1,0:T(8,128)S(1)} %shard_map.47), channel_id=1, source_target_pairs={{0,8},{1,9},{2,10},{3,11},{4,12},{5,13},{6,14},{7,15},{8,0},{9,1},... | collective-permute-start | bytes 3145736 | tf_op jit(solution)/shard_map/ppermute | solution.py:356
  17.9 63.1 %copy-start.2 = (s32[128]{0:T(128)S(1)}, s32[128]{0:T(128)}, u32[]{:S(2)}) copy-start(s32[128]{0:T(128)} %offsets.9) | copy-start | bytes 1540
  17.9 63.1 %copy-start.3 = (f32[128]{0:T(128)S(1)}, f32[128]{0:T(128)}, u32[]{:S(2)}) copy-start(f32[128]{0:T(128)} %weights.9) | copy-start | bytes 1540
  17.9 74.5 %collective-permute-start.8 = (f32[5,64,128]{2,1,0:T(8,128)S(1)}, f32[5,64,128]{2,1,0:T(8,128)S(1)}, u32[]{:S(2)}, u32[]{:S(2)}) collective-permute-start(f32[5,64,128]{2,1,0:T(8,128)S(1)} %shard_map.52), channel_id=1, source_target_pairs={{9,16},{10,17},{11,18},{12,19},{13,20},{14,21},{15,22},{17,8},{18,... | collective-permute-start | bytes 491528 | tf_op jit(solution)/shard_map/ppermute | solution.py:356
  44.5 47.8 %collective-permute-start.9 = (f32[5,64,128]{2,1,0:T(8,128)S(1)}, f32[5,64,128]{2,1,0:T(8,128)S(1)}, u32[]{:S(2)}, u32[]{:S(2)}) collective-permute-start(f32[5,64,128]{2,1,0:T(8,128)S(1)} %shard_map.53), channel_id=1, source_target_pairs={{0,8},{1,9},{2,10},{3,11},{4,12},{5,13},{6,14},{7,15},{8,0},{9,1},... | collective-permute-start | bytes 491528 | tf_op jit(solution)/shard_map/ppermute | solution.py:356
  66.5 34.9 %collective-permute-start.3 = (f32[5,64,128]{2,1,0:T(8,128)S(1)}, f32[5,64,128]{2,1,0:T(8,128)S(1)}, u32[]{:S(2)}, u32[]{:S(2)}) collective-permute-start(f32[5,64,128]{2,1,0:T(8,128)S(1)} %shard_map.48), channel_id=1, source_target_pairs={{8,17},{9,18},{10,19},{11,20},{12,21},{13,22},{14,23},{16,9},{17,1... | collective-permute-start | bytes 491528 | tf_op jit(solution)/shard_map/ppermute | solution.py:356
  81.0 20.4 %collective-permute-start.4 = (f32[5,64,128]{2,1,0:T(8,128)S(1)}, f32[5,64,128]{2,1,0:T(8,128)S(1)}, u32[]{:S(2)}, u32[]{:S(2)}) collective-permute-start(f32[5,64,128]{2,1,0:T(8,128)S(1)} %shard_map.49), channel_id=1, source_target_pairs={{0,8},{1,9},{2,10},{3,11},{4,12},{5,13},{6,14},{7,15},{8,0},{9,1},... | collective-permute-start | bytes 491528 | tf_op jit(solution)/shard_map/ppermute | solution.py:356
  111.5 50.4 %collective-permute-start.11 = (f32[4,16,64,128]{3,2,1,0:T(8,128)S(1)}, f32[4,16,64,128]{3,2,1,0:T(8,128)S(1)}, u32[]{:S(2)}, u32[]{:S(2)}) collective-permute-start(f32[4,16,64,128]{3,2,1,0:T(8,128)S(1)} %shard_map.55), channel_id=1, source_target_pairs={{0,8},{1,9},{2,10},{3,11},{4,12},{5,13},{6,14},{7,15},{8,0},{9,1},... | collective-permute-start | bytes 6291464 | tf_op jit(solution)/shard_map/ppermute | solution.py:356
  112.1 49.8 %collective-permute-start.6 = (f32[4,8,64,128]{3,2,1,0:T(8,128)S(1)}, f32[4,8,64,128]{3,2,1,0:T(8,128)S(1)}, u32[]{:S(2)}, u32[]{:S(2)}) collective-permute-start(f32[4,8,64,128]{3,2,1,0:T(8,128)S(1)} %get-tuple-element.12), channel_id=1, source_target_pairs={{8,16},{9,17},{10,18},{11,19},{12,20},{13,21},{14,22},{15,23},{16,... | collective-permute-start | bytes 3145736 | tf_op jit(solution)/shard_map/ppermute | solution.py:356
  114.0 42.3 %collective-permute-start.10 = (f32[4,4,64,128]{3,2,1,0:T(8,128)S(1)}, f32[4,4,64,128]{3,2,1,0:T(8,128)S(1)}, u32[]{:S(2)}, u32[]{:S(2)}) collective-permute-start(f32[4,4,64,128]{3,2,1,0:T(8,128)S(1)} %get-tuple-element.13), channel_id=1, source_target_pairs={{8,16},{9,17},{10,18},{11,19},{12,20},{13,21},{14,22},{15,23},{16,... | collective-permute-start | bytes 1572872 | tf_op jit(solution)/shard_map/ppermute | solution.py:356
  117.6 44.3 %copy-start.4 = (s32[16]{0:T(128)S(1)}, s32[16]{0:T(128)}, u32[]{:S(2)}) copy-start(s32[16]{0:T(128)} %counts.1) | copy-start | bytes 196
  117.7 44.2 %collective-permute-start.5 = (f32[4,4,64,128]{3,2,1,0:T(8,128)S(1)}, f32[4,4,64,128]{3,2,1,0:T(8,128)S(1)}, u32[]{:S(2)}, u32[]{:S(2)}) collective-permute-start(f32[4,4,64,128]{3,2,1,0:T(8,128)S(1)} %get-tuple-element.11), channel_id=1, source_target_pairs={{8,16},{9,17},{10,18},{11,19},{12,20},{13,21},{14,22},{15,23},{16,... | collective-permute-start | bytes 1572872 | tf_op jit(solution)/shard_map/ppermute | solution.py:356
where the time goes:
time: 164 us
  waiting for transfers between devices  92.2 us (56%)
  Pallas kernels  40.3 us (25%)
  starting transfers between devices  26.5 us (16%)
  local copies, waits for them, and re-layouts  4.91 us (3%)
    ppermute x12, waiting for transfers between devices, send(): return lax.ppermute(block, AXES, routes(segs, tiles, ds_of, dt))  92.2 us
    pallas_call x12, Pallas kernels, call(): return pl.pallas_call(kernel, **settings)(*args)  40.3 us
    ppermute x12, starting transfers between devices, send(): return lax.ppermute(block, AXES, routes(segs, tiles, ds_of, dt))  26.5 us
  transfers between devices with their start and end apart: 12, of which 5 were waited for; matrix products, arithmetic and copies ran while one was open for 0% of the time, Pallas kernels for 17%

commit v1 on v0

--- a/solution.py
+++ b/solution.py
@@ -88,36 +88,59 @@
     each_plane(images, planes, body)
 
 
-def descend(p, r, images, s, segs, outside):
-    n = p.shape[1]
+def descend(p, r, images, s, segs, ranges, rows, outside):
     first_id, last_id = s * images - 2, segs * images - 1
     for step in range(2):
-        lo, hi = 2 * step + 1, n - 2 * step - 1
-        residual_stage(p, r, (step, images + 3 - step), (lo, hi))
+        at, moved = ranges[step]
+        residual_rows, update_rows = rows[step]
+        residual_stage(p, r, residual_rows, at)
 
         @pl.when(s == 0)
         def _():
-            clear(r, (step, 2), (lo, hi))
+            clear(r, (step, 2), at)
 
         @pl.when(s == segs - 1)
         def _():
-            clear(r, (images + 1, images + 3 - step), (lo, hi))
+            clear(r, (images + 1, images + 3 - step), at)
 
         for cond, planes in outside:
 
             @pl.when(cond)
             def _(planes=planes):
-                clear(r, (step, images + 3 - step), planes)
-
-        update_stage(
-            p, r, (step + 1, images + 3 - step), (lo + 1, hi - 1), first_id, last_id
-        )
+                clear(r, residual_rows, planes)
+
+        update_stage(p, r, update_rows, moved, first_id, last_id)
         if step == 0:
             for cond, planes in outside:
 
                 @pl.when(cond)
                 def _(planes=planes):
-                    clear(p, (1, images + 3), planes)
+                    clear(p, update_rows, planes)
+
+
+def all_rows(images):
+    return (
+        ((0, images + 3), (1, images + 3)),
+        ((1, images + 2), (2, images + 2)),
+    )
+
+
+def inner_rows(images, core):
+    a = jnp.where(core == 0, 2, 0)
+    return (
+        ((a, a + images + 1), (a + 1, a + images + 1)),
+        ((a + 1, a + images), (a + 2, a + images)),
+    )
+
+
+def outer_rows(images, core):
+    starts = [jnp.where(core == 0, a, images + b) for a, b in ((0, 1), (1, 1), (1, 0), (2, 0))]
+    first, second, third, fourth = [(a, a + 2) for a in starts]
+    return ((first, second), (third, fourth))
+
+
+def inside_ranges(n):
+    return (((1, n - 1), (2, n - 2)), ((3, n - 3), (4, n - 4)))
 
 
 def mix(weights, offsets, k, p, base, x):
@@ -146,8 +169,30 @@
     return jnp.where(core == 0, (s + 1) * images, s * images - half)
 
 
-def inside_kernel(
-    segs, place, offsets, weights, path, from_outer, from_inner, p2, slots, p, r, sems
+def border_parts(p, r, n):
+    return (
+        p.at[:, pl.ds(2, 2)],
+        r.at[:, pl.ds(1, 4)],
+        p.at[:, pl.ds(n - 4, 2)],
+        r.at[:, pl.ds(n - 5, 4)],
+    )
+
+
+def inside_a_kernel(
+    segs,
+    place,
+    path,
+    from_inner,
+    p2,
+    p_low,
+    r_low,
+    p_high,
+    r_high,
+    p_kept,
+    r_kept,
+    p,
+    r,
+    sems,
 ):
     images, n = path.shape[0], path.shape[1]
     s = place[0]
@@ -156,14 +201,87 @@
         [
             pltpu.make_async_copy(path, p.at[pl.ds(2, images)], sems.at[0]),
             pltpu.make_async_copy(
-                from_outer, p.at[pl.ds(jnp.where(core == 0, 0, images + 2), 2)], sems.at[1]
+                from_inner, p.at[pl.ds(jnp.where(core == 0, images + 2, 0), 2)], sems.at[1]
+            ),
+        ]
+    )
+    descend(p, r, images, s, segs, inside_ranges(n), inner_rows(images, core), ())
+    p_row = jnp.where(core == 0, 2, images)
+    r_row = jnp.where(core == 0, 2, images - 1)
+    p2_row = jnp.where(core == 0, 2, 0)
+    plan = list(zip(border_parts(p, r, n), (p_low, r_low, p_high, r_high))) + [
+        (p.at[pl.ds(p_row, 2)], p_kept),
+        (r.at[pl.ds(r_row, 2)], r_kept),
+        (
+            p.at[pl.ds(p2_row + 2, images - 2), pl.ds(4, n - 8)],
+            p2.at[pl.ds(p2_row, images - 2)],
+        ),
+    ]
+    run_copies([pltpu.make_async_copy(a, b, sems.at[i]) for i, (a, b) in enumerate(plan)])
+
+
+def inside_b_kernel(
+    segs,
+    place,
+    offsets,
+    weights,
+    from_outer,
+    p_kept,
+    r_kept,
+    p2_in,
+    p_low_in,
+    r_low_in,
+    p_high_in,
+    r_high_in,
+    p2,
+    p_low,
+    r_low,
+    p_high,
+    r_high,
+    slots,
+    p,
+    r,
+    sems,
+):
+    del p_low_in, r_low_in, p_high_in, r_high_in
+    images, n = p2_in.shape[0], p_kept.shape[1]
+    s = place[0]
+    core = lax.rem(s, 2)
+    p2_row = jnp.where(core == 0, 2, 0)
+    done = pltpu.make_async_copy(
+        p2_in.at[pl.ds(p2_row, images - 2)],
+        p.at[pl.ds(p2_row + 2, images - 2), pl.ds(4, n - 8)],
+        sems.at[5],
+    )
+    done.start()
+    run_copies(
+        [
+            pltpu.make_async_copy(
+                from_outer, p.at[pl.ds(jnp.where(core == 0, 0, images + 2), 2)], sems.at[0]
             ),
             pltpu.make_async_copy(
-                from_inner, p.at[pl.ds(jnp.where(core == 0, images + 2, 0), 2)], sems.at[2]
+                p_kept, p.at[pl.ds(jnp.where(core == 0, 2, images), 2)], sems.at[1]
+            ),
+            pltpu.make_async_copy(
+                r_kept, r.at[pl.ds(jnp.where(core == 0, 2, images - 1), 2)], sems.at[2]
             ),
         ]
     )
-    descend(p, r, images, s, segs, ())
+    descend(p, r, images, s, segs, inside_ranges(n), outer_rows(images, core), ())
+    done.wait()
+    p_rows = pl.ds(jnp.where(core == 0, 0, images), 4)
+    r_rows = pl.ds(jnp.where(core == 0, 0, images), 3)
+    new_row = jnp.where(core == 0, 0, images - 2)
+    parts = border_parts(p, r, n)
+    plan = [
+        (part.at[rows], out.at[rows])
+        for part, out, rows in zip(
+            parts, (p_low, r_low, p_high, r_high), (p_rows, r_rows, p_rows, r_rows)
+        )
+    ] + [(p.at[pl.ds(new_row + 2, 2), pl.ds(4, n - 8)], p2.at[pl.ds(new_row, 2)])]
+    copies = [pltpu.make_async_copy(a, b, sems.at[i]) for i, (a, b) in enumerate(plan)]
+    for c in copies:
+        c.start()
     half = images // 2
     total = segs * images
     k0 = outer_base(s, images)
@@ -173,11 +291,8 @@
         slots[i, x] = mix(weights, offsets, k, p, 2, x + 4)
 
     each_plane((0, half), (0, n - 8), to_slots)
-
-    def to_p2(j, x):
-        p2[j, x] = p[j + 2, x + 4]
-
-    each_plane((0, images), (0, n - 8), to_p2)
+    for c in copies:
+        c.wait()
 
 
 def edge_kernel(
@@ -193,6 +308,8 @@
     beyond,
     corner_outer,
     corner_inner,
+    p_border,
+    r_border,
     p2,
     slots,
     p,
@@ -208,7 +325,7 @@
     inner_far = jnp.where(core == 0, images + 3, 0)
     outer_row = jnp.where(core == 0, 0, images + 2)
     inner_row = jnp.where(core == 0, images + 2, 0)
-    own, at = (pl.ds(0, 8), pl.ds(4, 8)) if low else (pl.ds(n - 8, 8), pl.ds(0, 8))
+    own, at = (pl.ds(0, 2), pl.ds(4, 2)) if low else (pl.ds(n - 2, 2), pl.ds(6, 2))
     three, two = (pl.ds(1, 3), pl.ds(2, 2)) if low else (pl.ds(8, 3), pl.ds(8, 2))
     plan = [
         (path.at[:, own], p.at[pl.ds(2, images), at]),
@@ -219,13 +336,18 @@
         (corner_outer.at[pl.ds(3, 2)], p.at[outer_far, two]),
         (corner_inner.at[pl.ds(0, 3)], p.at[inner_near, three]),
         (corner_inner.at[pl.ds(3, 2)], p.at[inner_far, two]),
+        (p_border, p.at[:, pl.ds(6 if low else 4, 2)]),
+        (r_border, r.at[:, pl.ds(5 if low else 3, 4)]),
     ]
     run_copies([pltpu.make_async_copy(a, b, sems.at[i]) for i, (a, b) in enumerate(plan)])
     half = images // 2
     total = segs * images
     k0 = outer_base(s, images)
     outside = (t == 0, (1, 4)) if low else (t == tiles - 1, (8, 11))
-    descend(p, r, images, s, segs, (outside,))
+    ranges = (((1, 5), (2, 6)), ((3, 7), (4, 8)))
+    if not low:
+        ranges = (((7, 11), (6, 10)), ((5, 9), (4, 8)))
+    descend(p, r, images, s, segs, ranges, all_rows(images), (outside,))
 
     def to_slots(i, x):
         k = jnp.minimum(k0 + i, total - 1)
@@ -394,24 +516,42 @@
     corner_below = send(corner(path_field, False, True), outer, 1)
     corner_above = send(corner(path_field, True, True), outer, -1)
 
-    p2_inside, slots_inside = call(
-        functools.partial(inside_kernel, segs),
+    border = (field(images + 4, 2, gy, gz), field(images + 3, 4, gy, gz))
+    levels = [
+        pltpu.VMEM((images + 4, n, gy, gz), jnp.float32),
+        pltpu.VMEM((images + 3, n, gy, gz), jnp.float32),
+        pltpu.SemaphoreType.DMA((7,)),
+    ]
+    *first, p_kept, r_kept = call(
+        functools.partial(inside_a_kernel, segs),
+        place,
+        path_field,
+        from_inner,
+        out_shape=(field(images, n - 8, gy, gz),)
+        + border * 2
+        + (field(2, n, gy, gz), field(2, n, gy, gz)),
+        in_specs=[SMEM, ANY, ANY],
+        out_specs=(ANY,) * 7,
+        scratch_shapes=levels,
+        compiler_params=params(14),
+        cost_estimate=cost(36 * 10, 8),
+    )
+    p2_inside, *borders, slots_inside = call(
+        functools.partial(inside_b_kernel, segs),
         place,
         offsets,
         weights,
-        path_field,
         from_outer,
-        from_inner,
-        out_shape=(field(images, n - 8, gy, gz), field(half, n - 8, gy, gz)),
-        in_specs=[SMEM, SMEM, SMEM, ANY, ANY, ANY],
-        out_specs=(VMEM, VMEM),
-        scratch_shapes=[
-            pltpu.VMEM((images + 4, n, gy, gz), jnp.float32),
-            pltpu.VMEM((images + 3, n, gy, gz), jnp.float32),
-            pltpu.SemaphoreType.DMA((3,)),
-        ],
-        compiler_params=params(18),
-        cost_estimate=cost(44 * 10, 8),
+        p_kept,
+        r_kept,
+        *first,
+        out_shape=(field(images, n - 8, gy, gz),) + border * 2 + (field(half, n - 8, gy, gz),),
+        in_specs=[SMEM, SMEM, SMEM] + [ANY] * 8,
+        out_specs=(ANY,) * 5 + (VMEM,),
+        input_output_aliases={6 + i: i for i in range(5)},
+        scratch_shapes=levels,
+        compiler_params=params(14),
+        cost_estimate=cost(9 * 10, 6),
     )
     got_inside = send(slots_inside, outer, 0)
 
@@ -428,13 +568,14 @@
             beyond,
             corner_outer,
             corner_inner,
+            *(borders[:2] if low else borders[2:]),
             out_shape=(field(images, 4, gy, gz), field(half, 4, gy, gz)),
-            in_specs=[SMEM, SMEM, SMEM] + [ANY] * 6,
+            in_specs=[SMEM, SMEM, SMEM] + [ANY] * 8,
             out_specs=(VMEM, VMEM),
             scratch_shapes=[
                 pltpu.VMEM((images + 4, 12, gy, gz), jnp.float32),
                 pltpu.VMEM((images + 3, 12, gy, gz), jnp.float32),
-                pltpu.SemaphoreType.DMA((8,)),
+                pltpu.SemaphoreType.DMA((10,)),
             ],
             compiler_params=params(14),
             cost_estimate=cost(28 * 10, 6),

time: 164 us -> 157 us (0.957)
  the two profiles are of different devices: /device:TPU:48 before, /device:TPU:17 now
where the time goes in v1:
time: 157 us; the launch traced here: 156 us
  waiting for transfers between devices  84.2 us (54%)
  Pallas kernels  37.8 us (24%)
  starting transfers between devices  29.1 us (19%)
  local copies, waits for them, and re-layouts  4.92 us (3%)
    ppermute x12, waiting for transfers between devices, send(): return lax.ppermute(block, AXES, routes(segs, tiles, ds_of, dt))  84.2 us
    pallas_call x13, Pallas kernels, call(): return pl.pallas_call(kernel, **settings)(*args)  37.8 us
    ppermute x12, starting transfers between devices, send(): return lax.ppermute(block, AXES, routes(segs, tiles, ds_of, dt))  29.1 us
  transfers between devices with their start and end apart: 12, of which 4 were waited for; matrix products, arithmetic and copies ran while one was open for 0% of the time, Pallas kernels for 18%

profile of v1, /device:TPU:17, one launch (start us, length us, event | category | flops | bytes accessed | tf_op | source)
XLA Modules:
  0.0 156.4 jit_solution(10139842770933212887)
XLA Ops:
  0.0 2.7 %fusion = (f32[8,4,64,128]{3,2,1,0:T(8,128)}, f32[8,4,64,128]{3,2,1,0:T(8,128)S(1)}) fusion(f32[8,16,64,128]{3,2,1,0:T(8,128)} %path.9), kind=kLoop, calls=%fused_computation.1 | loop fusion | bytes 4194304 | tf_op jit(solution)/shard_map/slice | solution.py:515
  2.7 1.3 collective-permute-start.7
  4.0 6.2 %collective-permute-start.2 = (f32[8,4,64,128]{3,2,1,0:T(8,128)S(1)}, f32[8,4,64,128]{3,2,1,0:T(8,128)S(1)}, u32[]{:S(2)}, u32[]{:S(2)}) collective-permute-start(f32[8,4,64,128]{3,2,1,0:T(8,128)S(1)} %get-tuple-element.40), channel_id=1, source_target_pairs={{0,1},{1,2},{2,3},{3,4},{4,5},{5,6},{6,7},{8,9},{9,10},{10,11},{11... | collective-permute-start | bytes 3145736 | tf_op jit(solution)/shard_map/ppermute | solution.py:478
  10.2 0.1 pad_add_fusion.place
  10.3 0.0 copy-start
  10.3 2.2 %copy-done = f32[8,16,64,128]{3,2,1,0:T(8,128)S(1)} copy-done((f32[8,16,64,128]{3,2,1,0:T(8,128)S(1)}, f32[8,16,64,128]{3,2,1,0:T(8,128)}, u32[]{:S(2)}) %copy-start) | copy-done | bytes 4194328
  12.5 0.6 shard_map.47
  13.1 0.0 copy-start.1
  13.1 1.0 collective-permute-start.1
  14.1 0.6 shard_map.46
  14.8 3.2 %collective-permute-start = (f32[2,16,64,128]{3,2,1,0:T(8,128)S(1)}, f32[2,16,64,128]{3,2,1,0:T(8,128)S(1)}, u32[]{:S(2)}, u32[]{:S(2)}) collective-permute-start(f32[2,16,64,128]{3,2,1,0:T(8,128)S(1)} %shard_map.46), channel_id=1, source_target_pairs={{8,16},{9,17},{10,18},{11,19},{12,20},{13,21},{14,22},{15,23},{16,... | collective-permute-start | bytes 3145736 | tf_op jit(solution)/shard_map/ppermute | solution.py:478
  18.0 0.0 copy-done.1
  18.0 0.8 shard_map.53
  18.8 1.3 collective-permute-start.8
  20.1 22.4 %collective-permute-done.7.src.beyond = f32[8,4,64,128]{3,2,1,0:T(8,128)S(1)} collective-permute-done((f32[8,4,64,128]{3,2,1,0:T(8,128)}, f32[8,4,64,128]{3,2,1,0:T(8,128)S(1)}, u32[]{:S(2)}, u32[]{:S(2)}) %collective-permute-start.7) | collective-permute-done | bytes 1048608 | tf_op jit(solution)/shard_map/ppermute | solution.py:478
  42.5 0.8 shard_map.54
  43.3 2.2 %collective-permute-start.9 = (f32[5,64,128]{2,1,0:T(8,128)S(1)}, f32[5,64,128]{2,1,0:T(8,128)S(1)}, u32[]{:S(2)}, u32[]{:S(2)}) collective-permute-start(f32[5,64,128]{2,1,0:T(8,128)S(1)} %shard_map.54), channel_id=1, source_target_pairs={{0,8},{1,9},{2,10},{3,11},{4,12},{5,13},{6,14},{7,15},{8,0},{9,1},... | collective-permute-start | bytes 491528 | tf_op jit(solution)/shard_map/ppermute | solution.py:478
  45.5 0.8 shard_map.48
  46.3 22.7 %collective-permute-done.2.src.beyond = f32[8,4,64,128]{3,2,1,0:T(8,128)S(1)} collective-permute-done((f32[8,4,64,128]{3,2,1,0:T(8,128)S(1)}, f32[8,4,64,128]{3,2,1,0:T(8,128)S(1)}, u32[]{:S(2)}, u32[]{:S(2)}) %collective-permute-start.2) | collective-permute-done | bytes 1048608 | tf_op jit(solution)/shard_map/ppermute | solution.py:478
  69.0 4.6 %collective-permute-start.3 = (f32[5,64,128]{2,1,0:T(8,128)S(1)}, f32[5,64,128]{2,1,0:T(8,128)S(1)}, u32[]{:S(2)}, u32[]{:S(2)}) collective-permute-start(f32[5,64,128]{2,1,0:T(8,128)S(1)} %shard_map.48), channel_id=1, source_target_pairs={{8,17},{9,18},{10,19},{11,20},{12,21},{13,22},{14,23},{16,9},{17,1... | collective-permute-start | bytes 491528 | tf_op jit(solution)/shard_map/ppermute | solution.py:478
  73.6 0.8 shard_map.49
  74.4 0.0 copy-start.2
  74.4 0.0 copy-start.3
  74.4 0.0 collective-permute-done.1.from_inner
  74.4 1.7 %collective-permute-start.4 = (f32[5,64,128]{2,1,0:T(8,128)S(1)}, f32[5,64,128]{2,1,0:T(8,128)S(1)}, u32[]{:S(2)}, u32[]{:S(2)}) collective-permute-start(f32[5,64,128]{2,1,0:T(8,128)S(1)} %shard_map.49), channel_id=1, source_target_pairs={{0,8},{1,9},{2,10},{3,11},{4,12},{5,13},{6,14},{7,15},{8,0},{9,1},... | collective-permute-start | bytes 491528 | tf_op jit(solution)/shard_map/ppermute | solution.py:478
  76.1 9.6 %shard_map.50 = (f32[8,8,64,128]{3,2,1,0:T(8,128)S(1)}, f32[12,2,64,128]{3,2,1,0:T(8,128)S(1)}, f32[11,4,64,128]{3,2,1,0:T(8,128)S(1)}, f32[12,2,64,128]{3,2,1,0...) custom-call(s32[2]{0:T(128)S(1)} %pad_add_fusion.place, ...), custom_call_target="tpu_custom_call" | custom-call | flops 176947200 | bytes 8388608 | tf_op jit(solution)/shard_map/pallas_call | solution.py:484
  85.7 0.0 collective-permute-done.from_outer
  85.7 0.0 copy-done.2
  85.8 0.0 copy-done.3
  85.8 3.5 %shard_map.51 = (f32[8,8,64,128]{3,2,1,0:T(8,128)S(1)}, f32[12,2,64,128]{3,2,1,0:T(8,128)S(1)}, f32[11,4,64,128]{3,2,1,0:T(8,128)S(1)}, f32[12,2,64,128]{3,2,1,0...) custom-call(s32[2]{0:T(128)S(1)} %pad_add_fusion.place, ...), custom_call_target="tpu_custom_call", output_to_operand_aliasing={{0}: (6, {}), {1}: (7, {}), {2}: (8, {}), {3}: (9, {}), {4}... | custom-call | flops 44236800 | bytes 6291456 | tf_op jit(solution)/shard_map/pallas_call | solution.py:484
  89.2 0.0 collective-permute-done.8.corner_outer
  89.2 0.0 collective-permute-done.9.corner_inner
  89.2 7.0 %shard_map.55 = (f32[8,4,64,128]{3,2,1,0:T(8,128)S(1)}, f32[4,4,64,128]{3,2,1,0:T(8,128)S(1)}) custom-call(s32[2]{0:T(128)S(1)} %pad_add_fusion.place, s32[128]{0:T(128)S(1)} %copy-done.2, f32[128]{0:T(128)S(1)} %copy-done.3, f32[8,16,64,128]{3,2,1,0:T(8,128)S(1)} %copy-done.1, f32[2,16,64,128]{3,2,1,0:T(8,128)S(1)} %collective-permute-done.from_outer, ...), custom_call_target="tpu_custom_call" | custom-call | flops 137625600 | bytes 6291456 | tf_op jit(solution)/shard_map/pallas_call | solution.py:484
  96.3 0.0 collective-permute-done.3.corner_outer
  96.3 0.0 collective-permute-done.4.corner_inner
  96.3 7.3 %shard_map.52 = (f32[8,4,64,128]{3,2,1,0:T(8,128)S(1)}, f32[4,4,64,128]{3,2,1,0:T(8,128)S(1)}) custom-call(s32[2]{0:T(128)S(1)} %pad_add_fusion.place, s32[128]{0:T(128)S(1)} %copy-done.2, f32[128]{0:T(128)S(1)} %copy-done.3, f32[8,16,64,128]{3,2,1,0:T(8,128)S(1)} %copy-done.1, f32[2,16,64,128]{3,2,1,0:T(8,128)S(1)} %collective-permute-done.from_outer, ...), custom_call_target="tpu_custom_call" | custom-call | flops 137625600 | bytes 6291456 | tf_op jit(solution)/shard_map/pallas_call | solution.py:484
  103.6 0.9 shard_map.56
  104.5 0.1 collective-permute-start.11
  104.6 1.9 %collective-permute-start.6 = (f32[4,8,64,128]{3,2,1,0:T(8,128)S(1)}, f32[4,8,64,128]{3,2,1,0:T(8,128)S(1)}, u32[]{:S(2)}, u32[]{:S(2)}) collective-permute-start(f32[4,8,64,128]{3,2,1,0:T(8,128)S(1)} %get-tuple-element.32), channel_id=1, source_target_pairs={{8,16},{9,17},{10,18},{11,19},{12,20},{13,21},{14,22},{15,23},{16,... | collective-permute-start | bytes 3145736 | tf_op jit(solution)/shard_map/ppermute | solution.py:478
  106.5 3.6 %collective-permute-start.10 = (f32[4,4,64,128]{3,2,1,0:T(8,128)S(1)}, f32[4,4,64,128]{3,2,1,0:T(8,128)S(1)}, u32[]{:S(2)}, u32[]{:S(2)}) collective-permute-start(f32[4,4,64,128]{3,2,1,0:T(8,128)S(1)} %get-tuple-element.35), channel_id=1, source_target_pairs={{8,16},{9,17},{10,18},{11,19},{12,20},{13,21},{14,22},{15,23},{16,... | collective-permute-start | bytes 1572872 | tf_op jit(solution)/shard_map/ppermute | solution.py:478
  110.2 0.0 copy-start.4
  110.2 1.9 %collective-permute-start.5 = (f32[4,4,64,128]{3,2,1,0:T(8,128)S(1)}, f32[4,4,64,128]{3,2,1,0:T(8,128)S(1)}, u32[]{:S(2)}, u32[]{:S(2)}) collective-permute-start(f32[4,4,64,128]{3,2,1,0:T(8,128)S(1)} %get-tuple-element.31), channel_id=1, source_target_pairs={{8,16},{9,17},{10,18},{11,19},{12,20},{13,21},{14,22},{15,23},{16,... | collective-permute-start | bytes 1572872 | tf_op jit(solution)/shard_map/ppermute | solution.py:478
  112.1 3.2 %shard_map.57.own = f32[8,16,64,128]{3,2,1,0:T(8,128)} custom-call(s32[2]{0:T(128)S(1)} %pad_add_fusion.place, s32[128]{0:T(128)S(1)} %copy-done.2, f32[128]{0:T(128)S(1)} %copy-done.3, f32[8,4,64,128]{3,2,1,0:T(8,128)S(1)} %get-tuple-element.36.low, f32[8,8,64,128]{3,2,1,0:T(8,128)S(1)} %get-tuple-element.37.inside, ...), custom_call_target="tpu_custom_call" | custom-call | flops 15728640 | bytes 8388608 | tf_op jit(solution)/shard_map/pallas_call | solution.py:484
  115.3 33.5 %collective-permute-done.10.high = f32[4,4,64,128]{3,2,1,0:T(8,128)S(1)} collective-permute-done((f32[4,4,64,128]{3,2,1,0:T(8,128)S(1)}, f32[4,4,64,128]{3,2,1,0:T(8,128)S(1)}, u32[]{:S(2)}, u32[]{:S(2)}) %collective-permute-start.10) | collective-permute-done | bytes 524320 | tf_op jit(solution)/shard_map/ppermute | solution.py:478
  148.8 5.6 %collective-permute-done.5.low = f32[4,4,64,128]{3,2,1,0:T(8,128)S(1)} collective-permute-done((f32[4,4,64,128]{3,2,1,0:T(8,128)S(1)}, f32[4,4,64,128]{3,2,1,0:T(8,128)S(1)}, u32[]{:S(2)}, u32[]{:S(2)}) %collective-permute-start.5) | collective-permute-done | bytes 524320 | tf_op jit(solution)/shard_map/ppermute | solution.py:478
  154.4 0.0 collective-permute-done.6.inside
  154.4 0.0 collective-permute-done.11.inner_part
  154.4 0.0 copy-done.4
  154.4 1.9 %shard_map.58 = f32[8,16,64,128]{3,2,1,0:T(8,128)} custom-call(s32[2]{0:T(128)S(1)} %pad_add_fusion.place, s32[16]{0:T(128)S(1)} %copy-done.4, f32[4,4,64,128]{3,2,1,0:T(8,128)S(1)} %collective-permute-done.5.low, f32[4,8,64,128]{3,2,1,0:T(8,128)S(1)} %collective-permute-done.6.inside, ...), custom_call_target="tpu_custom_call", output_to_operand_aliasing={{}: (6, {})} | custom-call | flops 983040 | bytes 4194304 | tf_op jit(solution)/shard_map/pallas_call | solution.py:484
Async XLA Ops:
  2.7 39.8 %collective-permute-start.7 = (f32[8,4,64,128]{3,2,1,0:T(8,128)}, f32[8,4,64,128]{3,2,1,0:T(8,128)S(1)}, u32[]{:S(2)}, u32[]{:S(2)}) collective-permute-start(f32[8,4,64,128]{3,2,1,0:T(8,128)} %get-tuple-element.39), channel_id=1, source_target_pairs={{1,0},{2,1},{3,2},{4,3},{5,4},{6,5},{7,6},{9,8},{10,9},{11,10},{12... | collective-permute-start | bytes 3145736 | tf_op jit(solution)/shard_map/ppermute | solution.py:478
  4.0 65.0 %collective-permute-start.2 = (f32[8,4,64,128]{3,2,1,0:T(8,128)S(1)}, f32[8,4,64,128]{3,2,1,0:T(8,128)S(1)}, u32[]{:S(2)}, u32[]{:S(2)}) collective-permute-start(f32[8,4,64,128]{3,2,1,0:T(8,128)S(1)} %get-tuple-element.40), channel_id=1, source_target_pairs={{0,1},{1,2},{2,3},{3,4},{4,5},{5,6},{6,7},{8,9},{9,10},{10,11},{11... | collective-permute-start | bytes 3145736 | tf_op jit(solution)/shard_map/ppermute | solution.py:478
  10.3 2.2 %copy-start = (f32[8,16,64,128]{3,2,1,0:T(8,128)S(1)}, f32[8,16,64,128]{3,2,1,0:T(8,128)}, u32[]{:S(2)}) copy-start(f32[8,16,64,128]{3,2,1,0:T(8,128)} %path.9) | copy-start | bytes 12582916
  13.1 4.9 %copy-start.1 = (f32[8,16,64,128]{3,2,1,0:T(8,128)S(1)}, f32[8,16,64,128]{3,2,1,0:T(8,128)}, u32[]{:S(2)}) copy-start(f32[8,16,64,128]{3,2,1,0:T(8,128)} %path.9) | copy-start | bytes 12582916
  13.1 61.3 %collective-permute-start.1 = (f32[2,16,64,128]{3,2,1,0:T(8,128)S(1)}, f32[2,16,64,128]{3,2,1,0:T(8,128)S(1)}, u32[]{:S(2)}, u32[]{:S(2)}) collective-permute-start(f32[2,16,64,128]{3,2,1,0:T(8,128)S(1)} %shard_map.47), channel_id=1, source_target_pairs={{0,8},{1,9},{2,10},{3,11},{4,12},{5,13},{6,14},{7,15},{8,0},{9,1},... | collective-permute-start | bytes 3145736 | tf_op jit(solution)/shard_map/ppermute | solution.py:478
  14.8 70.9 %collective-permute-start = (f32[2,16,64,128]{3,2,1,0:T(8,128)S(1)}, f32[2,16,64,128]{3,2,1,0:T(8,128)S(1)}, u32[]{:S(2)}, u32[]{:S(2)}) collective-permute-start(f32[2,16,64,128]{3,2,1,0:T(8,128)S(1)} %shard_map.46), channel_id=1, source_target_pairs={{8,16},{9,17},{10,18},{11,19},{12,20},{13,21},{14,22},{15,23},{16,... | collective-permute-start | bytes 3145736 | tf_op jit(solution)/shard_map/ppermute | solution.py:478
  18.8 70.4 %collective-permute-start.8 = (f32[5,64,128]{2,1,0:T(8,128)S(1)}, f32[5,64,128]{2,1,0:T(8,128)S(1)}, u32[]{:S(2)}, u32[]{:S(2)}) collective-permute-start(f32[5,64,128]{2,1,0:T(8,128)S(1)} %shard_map.53), channel_id=1, source_target_pairs={{9,16},{10,17},{11,18},{12,19},{13,20},{14,21},{15,22},{17,8},{18,... | collective-permute-start | bytes 491528 | tf_op jit(solution)/shard_map/ppermute | solution.py:478
  43.3 45.9 %collective-permute-start.9 = (f32[5,64,128]{2,1,0:T(8,128)S(1)}, f32[5,64,128]{2,1,0:T(8,128)S(1)}, u32[]{:S(2)}, u32[]{:S(2)}) collective-permute-start(f32[5,64,128]{2,1,0:T(8,128)S(1)} %shard_map.54), channel_id=1, source_target_pairs={{0,8},{1,9},{2,10},{3,11},{4,12},{5,13},{6,14},{7,15},{8,0},{9,1},... | collective-permute-start | bytes 491528 | tf_op jit(solution)/shard_map/ppermute | solution.py:478
  69.0 27.3 %collective-permute-start.3 = (f32[5,64,128]{2,1,0:T(8,128)S(1)}, f32[5,64,128]{2,1,0:T(8,128)S(1)}, u32[]{:S(2)}, u32[]{:S(2)}) collective-permute-start(f32[5,64,128]{2,1,0:T(8,128)S(1)} %shard_map.48), channel_id=1, source_target_pairs={{8,17},{9,18},{10,19},{11,20},{12,21},{13,22},{14,23},{16,9},{17,1... | collective-permute-start | bytes 491528 | tf_op jit(solution)/shard_map/ppermute | solution.py:478
  74.4 11.4 %copy-start.2 = (s32[128]{0:T(128)S(1)}, s32[128]{0:T(128)}, u32[]{:S(2)}) copy-start(s32[128]{0:T(128)} %offsets.9) | copy-start | bytes 1540
  74.4 11.4 %copy-start.3 = (f32[128]{0:T(128)S(1)}, f32[128]{0:T(128)}, u32[]{:S(2)}) copy-start(f32[128]{0:T(128)} %weights.9) | copy-start | bytes 1540
  74.4 21.9 %collective-permute-start.4 = (f32[5,64,128]{2,1,0:T(8,128)S(1)}, f32[5,64,128]{2,1,0:T(8,128)S(1)}, u32[]{:S(2)}, u32[]{:S(2)}) collective-permute-start(f32[5,64,128]{2,1,0:T(8,128)S(1)} %shard_map.49), channel_id=1, source_target_pairs={{0,8},{1,9},{2,10},{3,11},{4,12},{5,13},{6,14},{7,15},{8,0},{9,1},... | collective-permute-start | bytes 491528 | tf_op jit(solution)/shard_map/ppermute | solution.py:478
  104.5 49.9 %collective-permute-start.11 = (f32[4,16,64,128]{3,2,1,0:T(8,128)S(1)}, f32[4,16,64,128]{3,2,1,0:T(8,128)S(1)}, u32[]{:S(2)}, u32[]{:S(2)}) collective-permute-start(f32[4,16,64,128]{3,2,1,0:T(8,128)S(1)} %shard_map.56), channel_id=1, source_target_pairs={{0,8},{1,9},{2,10},{3,11},{4,12},{5,13},{6,14},{7,15},{8,0},{9,1},... | collective-permute-start | bytes 6291464 | tf_op jit(solution)/shard_map/ppermute | solution.py:478
  104.6 49.8 %collective-permute-start.6 = (f32[4,8,64,128]{3,2,1,0:T(8,128)S(1)}, f32[4,8,64,128]{3,2,1,0:T(8,128)S(1)}, u32[]{:S(2)}, u32[]{:S(2)}) collective-permute-start(f32[4,8,64,128]{3,2,1,0:T(8,128)S(1)} %get-tuple-element.32), channel_id=1, source_target_pairs={{8,16},{9,17},{10,18},{11,19},{12,20},{13,21},{14,22},{15,23},{16,... | collective-permute-start | bytes 3145736 | tf_op jit(solution)/shard_map/ppermute | solution.py:478
  106.5 42.3 %collective-permute-start.10 = (f32[4,4,64,128]{3,2,1,0:T(8,128)S(1)}, f32[4,4,64,128]{3,2,1,0:T(8,128)S(1)}, u32[]{:S(2)}, u32[]{:S(2)}) collective-permute-start(f32[4,4,64,128]{3,2,1,0:T(8,128)S(1)} %get-tuple-element.35), channel_id=1, source_target_pairs={{8,16},{9,17},{10,18},{11,19},{12,20},{13,21},{14,22},{15,23},{16,... | collective-permute-start | bytes 1572872 | tf_op jit(solution)/shard_map/ppermute | solution.py:478
  110.2 44.3 %copy-start.4 = (s32[16]{0:T(128)S(1)}, s32[16]{0:T(128)}, u32[]{:S(2)}) copy-start(s32[16]{0:T(128)} %counts.1) | copy-start | bytes 196
  110.2 44.2 %collective-permute-start.5 = (f32[4,4,64,128]{3,2,1,0:T(8,128)S(1)}, f32[4,4,64,128]{3,2,1,0:T(8,128)S(1)}, u32[]{:S(2)}, u32[]{:S(2)}) collective-permute-start(f32[4,4,64,128]{3,2,1,0:T(8,128)S(1)} %get-tuple-element.31), channel_id=1, source_target_pairs={{8,16},{9,17},{10,18},{11,19},{12,20},{13,21},{14,22},{15,23},{16,... | collective-permute-start | bytes 1572872 | tf_op jit(solution)/shard_map/ppermute | solution.py:478

commit v2 on v1

--- a/solution.py
+++ b/solution.py
@@ -14,16 +14,19 @@
 
 
 AXES = ("seg", "tile")
+BODY_PLANES = 16
 ANY = pl.BlockSpec(memory_space=pl.ANY)
 VMEM = pl.BlockSpec(memory_space=pltpu.VMEM)
 SMEM = pl.BlockSpec(memory_space=pltpu.SMEM)
 
 
-def routes(segs, tiles, ds_of, dt):
+def routes(segs, tiles, ds_of, dt_of):
     pairs = []
     for s in range(segs):
+        if ds_of(s) is None:
+            continue
         for t in range(tiles):
-            to_s, to_t = s + ds_of(s), t + dt
+            to_s, to_t = s + ds_of(s), t + dt_of(t)
             if 0 <= to_s < segs and 0 <= to_t < tiles:
                 pairs.append((s * tiles + t, to_s * tiles + to_t))
     return pairs
@@ -31,6 +34,14 @@
 
 def outer(s):
     return 1 if s % 2 else -1
+
+
+def along_y(s):
+    return outer(s) if s % 4 in (0, 3) else None
+
+
+def along_z(s):
+    return outer(s) if s % 4 in (1, 2) else None
 
 
 def inner(s):
@@ -45,14 +56,22 @@
 
 
 def each_plane(images, planes, body):
-    def over_images(j, carry):
-        def over_planes(x, inner_carry):
-            body(j, x)
-            return inner_carry
-
-        return lax.fori_loop(planes[0], planes[1], over_planes, carry, unroll=planes[1] - planes[0])
-
-    lax.fori_loop(images[0], images[1], over_images, 0)
+    first, count = images
+    width = planes[1] - planes[0]
+    group = max(1, min(count, BODY_PLANES // width))
+
+    def rows(start, size):
+        for j in range(size):
+            for x in range(*planes):
+                body(start + j, x)
+
+    def over_groups(i, carry):
+        rows(first + i * group, group)
+        return carry
+
+    lax.fori_loop(0, count // group, over_groups, 0)
+    if count % group:
+        rows(first + count - count % group, count % group)
 
 
 def residual_stage(p, r, images, planes):
@@ -97,11 +116,11 @@
 
         @pl.when(s == 0)
         def _():
-            clear(r, (step, 2), at)
+            clear(r, (step, 2 - step), at)
 
         @pl.when(s == segs - 1)
         def _():
-            clear(r, (images + 1, images + 3 - step), at)
+            clear(r, (images + 1, 2 - step), at)
 
         for cond, planes in outside:
 
@@ -120,22 +139,22 @@
 
 def all_rows(images):
     return (
-        ((0, images + 3), (1, images + 3)),
-        ((1, images + 2), (2, images + 2)),
+        ((0, images + 3), (1, images + 2)),
+        ((1, images + 1), (2, images)),
     )
 
 
 def inner_rows(images, core):
     a = jnp.where(core == 0, 2, 0)
     return (
-        ((a, a + images + 1), (a + 1, a + images + 1)),
-        ((a + 1, a + images), (a + 2, a + images)),
+        ((a, images + 1), (a + 1, images)),
+        ((a + 1, images - 1), (a + 2, images - 2)),
     )
 
 
 def outer_rows(images, core):
     starts = [jnp.where(core == 0, a, images + b) for a, b in ((0, 1), (1, 1), (1, 0), (2, 0))]
-    first, second, third, fourth = [(a, a + 2) for a in starts]
+    first, second, third, fourth = [(a, 2) for a in starts]
     return ((first, second), (third, fourth))
 
 
@@ -238,7 +257,8 @@
     r_low,
     p_high,
     r_high,
-    slots,
+    slots_near,
+    slots_far,
     p,
     r,
     sems,
@@ -282,15 +302,18 @@
     copies = [pltpu.make_async_copy(a, b, sems.at[i]) for i, (a, b) in enumerate(plan)]
     for c in copies:
         c.start()
-    half = images // 2
+    quarter = images // 4
     total = segs * images
-    k0 = outer_base(s, images)
-
-    def to_slots(i, x):
-        k = jnp.minimum(k0 + i, total - 1)
-        slots[i, x] = mix(weights, offsets, k, p, 2, x + 4)
-
-    each_plane((0, half), (0, n - 8), to_slots)
+    for slots, k0 in (
+        (slots_near, outer_base(s, images)),
+        (slots_far, outer_base(s, images) + quarter),
+    ):
+
+        def to_slots(i, x, slots=slots, k0=k0):
+            k = jnp.minimum(k0 + i, total - 1)
+            slots[i, x] = mix(weights, offsets, k, p, 2, x + 4)
+
+        each_plane((0, quarter), (0, n - 8), to_slots)
     for c in copies:
         c.wait()
 
@@ -411,42 +434,68 @@
         each_plane((0, images), (0, hi - lo), body)
 
 
-def source_step(counts, k, s, segs):
+def bounds(segs, counts, s):
+    before = jnp.int32(0)
     end = jnp.int32(0)
-    source = jnp.int32(0)
     for i in range(segs):
-        end = end + counts[i]
-        source = source + jnp.where(end <= k, 1, 0)
-    return source - s
-
-
-def place_kernel(segs, place, counts, low, inside, high, inner_part, own, out, sems):
+        before = before + jnp.where(i < s, counts[i], 0)
+        end = end + jnp.where(i <= s, counts[i], 0)
+    return before, end
+
+
+def choose_kernel(segs, place, counts, near, lent, out, sems):
+    s = place[0]
+    images = 4 * near.shape[0]
+    before, end = bounds(segs, counts, s)
+    gives = jnp.where(lax.rem(s, 2) == 0, before < s * images, end > (s + 1) * images)
+    gives = gives | (lax.rem(lax.div(s + 1, 2), 2) == 1)
+
+    @pl.when(gives)
+    def _():
+        run_copies([pltpu.make_async_copy(near, out, sems.at[0])])
+
+    @pl.when(jnp.logical_not(gives))
+    def _():
+        run_copies([pltpu.make_async_copy(lent, out, sems.at[0])])
+
+
+def place_kernel(
+    segs, place, counts, low, near, far, back, high, inner_part, own, out, sems
+):
     del own
     images, n = out.shape[0], out.shape[1]
     half = images // 2
+    quarter = half // 2
     s = place[0]
     core = lax.rem(s, 2)
-
-    def copies(i, slot, from_outer):
+    before, end = bounds(segs, counts, s)
+    is_z = lax.rem(lax.div(s + 1, 2), 2) == 1
+
+    def copies(i, slot, from_outer, rest):
         for lo, hi, which in plane_parts(n):
             if from_outer:
-                src = (low, inside, high)[which].at[slot]
+                inside = near if slot < quarter else rest
+                row = slot if which != 1 else slot % quarter
+                src = (low, inside, high)[which].at[row]
             else:
                 src = inner_part.at[slot, pl.ds(lo, hi - lo)]
             yield pltpu.make_async_copy(src, out.at[i, pl.ds(lo, hi - lo)], sems.at[i, which])
 
     for start in (True, False):
         for i in range(images):
-            step = source_step(counts, s * images + i, s, segs)
+            k = s * images + i
             slot = i % half
-            foreign = (step < 0) if i < half else (step > 0)
+            foreign = (k < before) if i < half else (k >= end)
             outer_core = 0 if i < half else 1
 
-            for from_outer in (True, False):
-
-                @pl.when(foreign & ((core == outer_core) == from_outer))
-                def _(i=i, slot=slot, from_outer=from_outer):
-                    for c in copies(i, slot, from_outer):
+            cases = [((core == outer_core) & is_z, True, far)]
+            cases += [((core == outer_core) & jnp.logical_not(is_z), True, back)]
+            cases += [(core != outer_core, False, None)]
+            for cond, from_outer, rest in cases:
+
+                @pl.when(foreign & cond)
+                def _(i=i, slot=slot, from_outer=from_outer, rest=rest):
+                    for c in copies(i, slot, from_outer, rest):
                         if start:
                             c.start()
                         else:
@@ -475,7 +524,11 @@
     place = jnp.stack([s, t]).astype(jnp.int32)
 
     def send(block, ds_of, dt):
-        return lax.ppermute(block, AXES, routes(segs, tiles, ds_of, dt))
+        dt_of = dt if callable(dt) else lambda _: dt
+        return lax.ppermute(block, AXES, routes(segs, tiles, ds_of, dt_of))
+
+    def across(tile):
+        return -1 if tile % 2 else 1
 
     def stay(_):
         return 0
@@ -536,7 +589,7 @@
         compiler_params=params(14),
         cost_estimate=cost(36 * 10, 8),
     )
-    p2_inside, *borders, slots_inside = call(
+    p2_inside, *borders, slots_near, slots_far = call(
         functools.partial(inside_b_kernel, segs),
         place,
         offsets,
@@ -545,15 +598,31 @@
         p_kept,
         r_kept,
         *first,
-        out_shape=(field(images, n - 8, gy, gz),) + border * 2 + (field(half, n - 8, gy, gz),),
+        out_shape=(field(images, n - 8, gy, gz),) + border * 2 + (field(half // 2, n - 8, gy, gz),) * 2,
         in_specs=[SMEM, SMEM, SMEM] + [ANY] * 8,
-        out_specs=(ANY,) * 5 + (VMEM,),
+        out_specs=(ANY,) * 5 + (VMEM,) * 2,
         input_output_aliases={6 + i: i for i in range(5)},
         scratch_shapes=levels,
         compiler_params=params(14),
         cost_estimate=cost(9 * 10, 6),
     )
-    got_inside = send(slots_inside, outer, 0)
+    lent = send(slots_far, along_y, across)
+    chosen = call(
+        functools.partial(choose_kernel, segs),
+        place,
+        counts,
+        slots_near,
+        lent,
+        out_shape=field(half // 2, n - 8, gy, gz),
+        in_specs=[SMEM, SMEM, ANY, ANY],
+        out_specs=VMEM,
+        scratch_shapes=[pltpu.SemaphoreType.DMA((1,))],
+        compiler_params=params(1),
+        cost_estimate=cost(0, 1),
+    )
+    got_near = send(chosen, outer, 0)
+    got_far = send(slots_far, along_z, 0)
+    got_back = send(got_near, along_y, across)
 
     def edge(low, beyond, corner_outer):
         corner_inner = send(corner(beyond, not low, False), inner, 0)
@@ -620,15 +689,17 @@
         place,
         counts,
         got_low,
-        got_inside,
+        got_near,
+        got_far,
+        got_back,
         got_high,
         got_inner,
         own,
         out_shape=field(images, n, gy, gz),
-        in_specs=[SMEM, SMEM, VMEM, VMEM, VMEM, VMEM, ANY],
+        in_specs=[SMEM, SMEM] + [VMEM] * 6 + [ANY],
         out_specs=ANY,
         scratch_shapes=[pltpu.SemaphoreType.DMA((images, 3))],
-        input_output_aliases={6: 0},
+        input_output_aliases={8: 0},
         compiler_params=params(6),
         cost_estimate=cost(2, 4),
     )

time: 157 us -> 148 us (0.943)
  waiting for transfers between devices: 84.2 us -> 74.4 us
  starting transfers between devices: 29.1 us -> 34.1 us
  Pallas kernels: 37.8 us -> 33.8 us
    ppermute x12 -> x15, waiting for transfers between devices: 84.2 us -> 74.4 us  [send(): return lax.ppermute(block, AXES, routes(segs, tiles, ds_of, dt_of))]
    ppermute x12 -> x15, starting transfers between devices: 29.1 us -> 34.1 us  [send(): return lax.ppermute(block, AXES, routes(segs, tiles, ds_of, dt_of))]
    pallas_call x13 -> x14, Pallas kernels: 37.8 us -> 33.8 us  [call(): return pl.pallas_call(kernel, **settings)(*args)]
  transfers between devices with their start and end apart: 12 -> 15, of which waited for: 4 -> 5; matrix products, arithmetic and copies ran while one was open for 0% -> 0% of each run, Pallas kernels for 18% -> 18%
where the time goes in v2:
time: 148 us
  waiting for transfers between devices  74.4 us (50%)
  starting transfers between devices  34.1 us (23%)
  Pallas kernels  33.8 us (23%)
  local copies, waits for them, and re-layouts  4.92 us (3%)
    ppermute x15, waiting for transfers between devices, send(): return lax.ppermute(block, AXES, routes(segs, tiles, ds_of, dt_of))  74.4 us
    ppermute x15, starting transfers between devices, send(): return lax.ppermute(block, AXES, routes(segs, tiles, ds_of, dt_of))  34.1 us
    pallas_call x14, Pallas kernels, call(): return pl.pallas_call(kernel, **settings)(*args)  33.8 us
  transfers between devices with their start and end apart: 15, of which 5 were waited for; matrix products, arithmetic and copies ran while one was open for 0% of the time, Pallas kernels for 18%

profile of v2, /device:TPU:17, one launch (start us, length us, event | category | flops | bytes accessed | tf_op | source)
XLA Modules:
  0.0 147.6 jit_solution(6635791206096168602)
XLA Ops:
  0.0 2.7 %fusion = (f32[8,4,64,128]{3,2,1,0:T(8,128)}, f32[8,4,64,128]{3,2,1,0:T(8,128)S(1)}) fusion(f32[8,16,64,128]{3,2,1,0:T(8,128)} %path.9), kind=kLoop, calls=%fused_computation.1 | loop fusion | bytes 4194304 | tf_op jit(solution)/shard_map/slice | solution.py:568
  2.7 1.3 collective-permute-start.10
  4.0 6.2 %collective-permute-start.2 = (f32[8,4,64,128]{3,2,1,0:T(8,128)S(1)}, f32[8,4,64,128]{3,2,1,0:T(8,128)S(1)}, u32[]{:S(2)}, u32[]{:S(2)}) collective-permute-start(f32[8,4,64,128]{3,2,1,0:T(8,128)S(1)} %get-tuple-element.42), channel_id=1, source_target_pairs={{0,1},{1,2},{2,3},{3,4},{4,5},{5,6},{6,7},{8,9},{9,10},{10,11},{11... | collective-permute-start | bytes 3145736 | tf_op jit(solution)/shard_map/ppermute | solution.py:528
  10.2 0.1 pad_add_fusion.place
  10.3 0.0 copy-start
  10.3 2.2 %copy-done = f32[8,16,64,128]{3,2,1,0:T(8,128)S(1)} copy-done((f32[8,16,64,128]{3,2,1,0:T(8,128)S(1)}, f32[8,16,64,128]{3,2,1,0:T(8,128)}, u32[]{:S(2)}) %copy-start) | copy-done | bytes 4194328
  12.5 0.6 shard_map.47
  13.1 0.0 copy-start.1
  13.1 1.0 collective-permute-start.1
  14.1 0.6 shard_map.46
  14.8 3.2 %collective-permute-start = (f32[2,16,64,128]{3,2,1,0:T(8,128)S(1)}, f32[2,16,64,128]{3,2,1,0:T(8,128)S(1)}, u32[]{:S(2)}, u32[]{:S(2)}) collective-permute-start(f32[2,16,64,128]{3,2,1,0:T(8,128)S(1)} %shard_map.46), channel_id=1, source_target_pairs={{8,16},{9,17},{10,18},{11,19},{12,20},{13,21},{14,22},{15,23},{16,... | collective-permute-start | bytes 3145736 | tf_op jit(solution)/shard_map/ppermute | solution.py:528
  18.0 0.0 copy-done.1
  18.0 0.8 shard_map.54
  18.8 1.3 collective-permute-start.11
  20.1 22.4 %collective-permute-done.10.src.beyond = f32[8,4,64,128]{3,2,1,0:T(8,128)S(1)} collective-permute-done((f32[8,4,64,128]{3,2,1,0:T(8,128)}, f32[8,4,64,128]{3,2,1,0:T(8,128)S(1)}, u32[]{:S(2)}, u32[]{:S(2)}) %collective-permute-start.10) | collective-permute-done | bytes 1048608 | tf_op jit(solution)/shard_map/ppermute | solution.py:528
  42.5 0.8 shard_map.55
  43.3 2.2 %collective-permute-start.12 = (f32[5,64,128]{2,1,0:T(8,128)S(1)}, f32[5,64,128]{2,1,0:T(8,128)S(1)}, u32[]{:S(2)}, u32[]{:S(2)}) collective-permute-start(f32[5,64,128]{2,1,0:T(8,128)S(1)} %shard_map.55), channel_id=1, source_target_pairs={{0,8},{1,9},{2,10},{3,11},{4,12},{5,13},{6,14},{7,15},{8,0},{9,1},... | collective-permute-start | bytes 491528 | tf_op jit(solution)/shard_map/ppermute | solution.py:528
  45.5 0.8 shard_map.48
  46.3 22.7 %collective-permute-done.2.src.beyond = f32[8,4,64,128]{3,2,1,0:T(8,128)S(1)} collective-permute-done((f32[8,4,64,128]{3,2,1,0:T(8,128)S(1)}, f32[8,4,64,128]{3,2,1,0:T(8,128)S(1)}, u32[]{:S(2)}, u32[]{:S(2)}) %collective-permute-start.2) | collective-permute-done | bytes 1048608 | tf_op jit(solution)/shard_map/ppermute | solution.py:528
  69.0 4.6 %collective-permute-start.3 = (f32[5,64,128]{2,1,0:T(8,128)S(1)}, f32[5,64,128]{2,1,0:T(8,128)S(1)}, u32[]{:S(2)}, u32[]{:S(2)}) collective-permute-start(f32[5,64,128]{2,1,0:T(8,128)S(1)} %shard_map.48), channel_id=1, source_target_pairs={{8,17},{9,18},{10,19},{11,20},{12,21},{13,22},{14,23},{16,9},{17,1... | collective-permute-start | bytes 491528 | tf_op jit(solution)/shard_map/ppermute | solution.py:528
  73.6 0.8 shard_map.49
  74.4 0.0 copy-start.2
  74.4 0.0 copy-start.3
  74.4 0.0 collective-permute-done.1.from_inner
  74.4 1.7 %collective-permute-start.4 = (f32[5,64,128]{2,1,0:T(8,128)S(1)}, f32[5,64,128]{2,1,0:T(8,128)S(1)}, u32[]{:S(2)}, u32[]{:S(2)}) collective-permute-start(f32[5,64,128]{2,1,0:T(8,128)S(1)} %shard_map.49), channel_id=1, source_target_pairs={{0,8},{1,9},{2,10},{3,11},{4,12},{5,13},{6,14},{7,15},{8,0},{9,1},... | collective-permute-start | bytes 491528 | tf_op jit(solution)/shard_map/ppermute | solution.py:528
  76.1 9.3 %shard_map.50 = (f32[8,8,64,128]{3,2,1,0:T(8,128)S(1)}, f32[12,2,64,128]{3,2,1,0:T(8,128)S(1)}, f32[11,4,64,128]{3,2,1,0:T(8,128)S(1)}, f32[12,2,64,128]{3,2,1,0...) custom-call(s32[2]{0:T(128)S(1)} %pad_add_fusion.place, ...), custom_call_target="tpu_custom_call" | custom-call | flops 176947200 | bytes 8388608 | tf_op jit(solution)/shard_map/pallas_call | solution.py:537
  85.5 0.0 collective-permute-done.from_outer
  85.5 0.0 copy-done.2
  85.5 0.0 copy-done.3
  85.5 3.3 %shard_map.51 = (f32[8,8,64,128]{3,2,1,0:T(8,128)S(1)}, f32[12,2,64,128]{3,2,1,0:T(8,128)S(1)}, f32[11,4,64,128]{3,2,1,0:T(8,128)S(1)}, f32[12,2,64,128]{3,2,1,0...) custom-call(s32[2]{0:T(128)S(1)} %pad_add_fusion.place, ...), custom_call_target="tpu_custom_call", output_to_operand_aliasing={{0}: (6, {}), {1}: (7, {}), {2}: (8, {}), {3}: (9, {}), {4}... | custom-call | flops 44236800 | bytes 6291456 | tf_op jit(solution)/shard_map/pallas_call | solution.py:537
  88.8 0.0 collective-permute-done.11.corner_outer
  88.8 0.0 collective-permute-done.12.corner_inner
  88.8 5.1 %shard_map.56 = (f32[8,4,64,128]{3,2,1,0:T(8,128)S(1)}, f32[4,4,64,128]{3,2,1,0:T(8,128)S(1)}) custom-call(s32[2]{0:T(128)S(1)} %pad_add_fusion.place, s32[128]{0:T(128)S(1)} %copy-done.2, f32[128]{0:T(128)S(1)} %copy-done.3, f32[8,16,64,128]{3,2,1,0:T(8,128)S(1)} %copy-done.1, f32[2,16,64,128]{3,2,1,0:T(8,128)S(1)} %collective-permute-done.from_outer, ...), custom_call_target="tpu_custom_call" | custom-call | flops 137625600 | bytes 6291456 | tf_op jit(solution)/shard_map/pallas_call | solution.py:537
  93.9 0.0 collective-permute-done.3.corner_outer
  93.9 0.0 collective-permute-done.4.corner_inner
  93.9 5.3 %shard_map.52 = (f32[8,4,64,128]{3,2,1,0:T(8,128)S(1)}, f32[4,4,64,128]{3,2,1,0:T(8,128)S(1)}) custom-call(s32[2]{0:T(128)S(1)} %pad_add_fusion.place, s32[128]{0:T(128)S(1)} %copy-done.2, f32[128]{0:T(128)S(1)} %copy-done.3, f32[8,16,64,128]{3,2,1,0:T(8,128)S(1)} %copy-done.1, f32[2,16,64,128]{3,2,1,0:T(8,128)S(1)} %collective-permute-done.from_outer, ...), custom_call_target="tpu_custom_call" | custom-call | flops 137625600 | bytes 6291456 | tf_op jit(solution)/shard_map/pallas_call | solution.py:537
  99.2 0.0 copy-start.4
  99.2 0.8 shard_map.57
  100.0 0.1 collective-permute-start.14
  100.1 0.7 collective-permute-start.6
  100.8 0.0 collective-permute-done.6.lent
  100.9 0.0 copy-done.4
  100.9 0.6 shard_map.53
  101.5 1.9 %collective-permute-start.7 = (f32[2,8,64,128]{3,2,1,0:T(8,128)S(1)}, f32[2,8,64,128]{3,2,1,0:T(8,128)S(1)}, u32[]{:S(2)}, u32[]{:S(2)}) collective-permute-start(f32[2,8,64,128]{3,2,1,0:T(8,128)S(1)} %shard_map.53), channel_id=1, source_target_pairs={{8,16},{9,17},{10,18},{11,19},{12,20},{13,21},{14,22},{15,23},{16,... | collective-permute-start | bytes 1572872 | tf_op jit(solution)/shard_map/ppermute | solution.py:528
  103.4 3.6 %collective-permute-start.8 = (f32[2,8,64,128]{3,2,1,0:T(8,128)S(1)}, f32[2,8,64,128]{3,2,1,0:T(8,128)S(1)}, u32[]{:S(2)}, u32[]{:S(2)}) collective-permute-start(f32[2,8,64,128]{3,2,1,0:T(8,128)S(1)} %get-tuple-element.34), channel_id=1, source_target_pairs={{8,16},{9,17},{10,18},{11,19},{12,20},{13,21},{14,22},{15,23},{16,... | collective-permute-start | bytes 1572872 | tf_op jit(solution)/shard_map/ppermute | solution.py:528
  107.1 1.9 %collective-permute-start.13 = (f32[4,4,64,128]{3,2,1,0:T(8,128)S(1)}, f32[4,4,64,128]{3,2,1,0:T(8,128)S(1)}, u32[]{:S(2)}, u32[]{:S(2)}) collective-permute-start(f32[4,4,64,128]{3,2,1,0:T(8,128)S(1)} %get-tuple-element.37), channel_id=1, source_target_pairs={{8,16},{9,17},{10,18},{11,19},{12,20},{13,21},{14,22},{15,23},{16,... | collective-permute-start | bytes 1572872 | tf_op jit(solution)/shard_map/ppermute | solution.py:528
  109.0 3.6 %collective-permute-start.5 = (f32[4,4,64,128]{3,2,1,0:T(8,128)S(1)}, f32[4,4,64,128]{3,2,1,0:T(8,128)S(1)}, u32[]{:S(2)}, u32[]{:S(2)}) collective-permute-start(f32[4,4,64,128]{3,2,1,0:T(8,128)S(1)} %get-tuple-element.32), channel_id=1, source_target_pairs={{8,16},{9,17},{10,18},{11,19},{12,20},{13,21},{14,22},{15,23},{16,... | collective-permute-start | bytes 1572872 | tf_op jit(solution)/shard_map/ppermute | solution.py:528
  112.7 0.0 collective-permute-done.7.near
  112.7 0.7 collective-permute-start.9
  113.4 3.1 %shard_map.58.own = f32[8,16,64,128]{3,2,1,0:T(8,128)} custom-call(s32[2]{0:T(128)S(1)} %pad_add_fusion.place, s32[128]{0:T(128)S(1)} %copy-done.2, f32[128]{0:T(128)S(1)} %copy-done.3, f32[8,4,64,128]{3,2,1,0:T(8,128)S(1)} %get-tuple-element.38.low, f32[8,8,64,128]{3,2,1,0:T(8,128)S(1)} %get-tuple-element.39.inside, ...), custom_call_target="tpu_custom_call" | custom-call | flops 15728640 | bytes 8388608 | tf_op jit(solution)/shard_map/pallas_call | solution.py:537
  116.5 1.2 collective-permute-done.8.far
  117.6 22.5 %collective-permute-done.13.high = f32[4,4,64,128]{3,2,1,0:T(8,128)S(1)} collective-permute-done((f32[4,4,64,128]{3,2,1,0:T(8,128)S(1)}, f32[4,4,64,128]{3,2,1,0:T(8,128)S(1)}, u32[]{:S(2)}, u32[]{:S(2)}) %collective-permute-start.13) | collective-permute-done | bytes 524320 | tf_op jit(solution)/shard_map/ppermute | solution.py:528
  140.1 5.6 %collective-permute-done.5.low = f32[4,4,64,128]{3,2,1,0:T(8,128)S(1)} collective-permute-done((f32[4,4,64,128]{3,2,1,0:T(8,128)S(1)}, f32[4,4,64,128]{3,2,1,0:T(8,128)S(1)}, u32[]{:S(2)}, u32[]{:S(2)}) %collective-permute-start.5) | collective-permute-done | bytes 524320 | tf_op jit(solution)/shard_map/ppermute | solution.py:528
  145.7 0.0 collective-permute-done.9.back
  145.7 0.0 collective-permute-done.14.inner_part
  145.7 1.8 %shard_map.59 = f32[8,16,64,128]{3,2,1,0:T(8,128)} custom-call(s32[2]{0:T(128)S(1)} %pad_add_fusion.place, s32[16]{0:T(128)S(1)} %copy-done.4, f32[4,4,64,128]{3,2,1,0:T(8,128)S(1)} %collective-permute-done.5.low, f32[2,8,64,128]{3,2,1,0:T(8,128)S(1)} %collective-permute-done.7.near, ...), custom_call_target="tpu_custom_call", output_to_operand_aliasing={{}: (8, {})} | custom-call | flops 983040 | bytes 4194304 | tf_op jit(solution)/shard_map/pallas_call | solution.py:537
Async XLA Ops:
  2.7 39.8 %collective-permute-start.10 = (f32[8,4,64,128]{3,2,1,0:T(8,128)}, f32[8,4,64,128]{3,2,1,0:T(8,128)S(1)}, u32[]{:S(2)}, u32[]{:S(2)}) collective-permute-start(f32[8,4,64,128]{3,2,1,0:T(8,128)} %get-tuple-element.41), channel_id=1, source_target_pairs={{1,0},{2,1},{3,2},{4,3},{5,4},{6,5},{7,6},{9,8},{10,9},{11,10},{12... | collective-permute-start | bytes 3145736 | tf_op jit(solution)/shard_map/ppermute | solution.py:528
  4.0 65.0 %collective-permute-start.2 = (f32[8,4,64,128]{3,2,1,0:T(8,128)S(1)}, f32[8,4,64,128]{3,2,1,0:T(8,128)S(1)}, u32[]{:S(2)}, u32[]{:S(2)}) collective-permute-start(f32[8,4,64,128]{3,2,1,0:T(8,128)S(1)} %get-tuple-element.42), channel_id=1, source_target_pairs={{0,1},{1,2},{2,3},{3,4},{4,5},{5,6},{6,7},{8,9},{9,10},{10,11},{11... | collective-permute-start | bytes 3145736 | tf_op jit(solution)/shard_map/ppermute | solution.py:528
  10.3 2.2 %copy-start = (f32[8,16,64,128]{3,2,1,0:T(8,128)S(1)}, f32[8,16,64,128]{3,2,1,0:T(8,128)}, u32[]{:S(2)}) copy-start(f32[8,16,64,128]{3,2,1,0:T(8,128)} %path.9) | copy-start | bytes 12582916
  13.1 4.9 %copy-start.1 = (f32[8,16,64,128]{3,2,1,0:T(8,128)S(1)}, f32[8,16,64,128]{3,2,1,0:T(8,128)}, u32[]{:S(2)}) copy-start(f32[8,16,64,128]{3,2,1,0:T(8,128)} %path.9) | copy-start | bytes 12582916
  13.1 61.3 %collective-permute-start.1 = (f32[2,16,64,128]{3,2,1,0:T(8,128)S(1)}, f32[2,16,64,128]{3,2,1,0:T(8,128)S(1)}, u32[]{:S(2)}, u32[]{:S(2)}) collective-permute-start(f32[2,16,64,128]{3,2,1,0:T(8,128)S(1)} %shard_map.47), channel_id=1, source_target_pairs={{0,8},{1,9},{2,10},{3,11},{4,12},{5,13},{6,14},{7,15},{8,0},{9,1},... | collective-permute-start | bytes 3145736 | tf_op jit(solution)/shard_map/ppermute | solution.py:528
  14.8 70.7 %collective-permute-start = (f32[2,16,64,128]{3,2,1,0:T(8,128)S(1)}, f32[2,16,64,128]{3,2,1,0:T(8,128)S(1)}, u32[]{:S(2)}, u32[]{:S(2)}) collective-permute-start(f32[2,16,64,128]{3,2,1,0:T(8,128)S(1)} %shard_map.46), channel_id=1, source_target_pairs={{8,16},{9,17},{10,18},{11,19},{12,20},{13,21},{14,22},{15,23},{16,... | collective-permute-start | bytes 3145736 | tf_op jit(solution)/shard_map/ppermute | solution.py:528
  18.8 70.0 %collective-permute-start.11 = (f32[5,64,128]{2,1,0:T(8,128)S(1)}, f32[5,64,128]{2,1,0:T(8,128)S(1)}, u32[]{:S(2)}, u32[]{:S(2)}) collective-permute-start(f32[5,64,128]{2,1,0:T(8,128)S(1)} %shard_map.54), channel_id=1, source_target_pairs={{9,16},{10,17},{11,18},{12,19},{13,20},{14,21},{15,22},{17,8},{18,... | collective-permute-start | bytes 491528 | tf_op jit(solution)/shard_map/ppermute | solution.py:528
  43.3 45.5 %collective-permute-start.12 = (f32[5,64,128]{2,1,0:T(8,128)S(1)}, f32[5,64,128]{2,1,0:T(8,128)S(1)}, u32[]{:S(2)}, u32[]{:S(2)}) collective-permute-start(f32[5,64,128]{2,1,0:T(8,128)S(1)} %shard_map.55), channel_id=1, source_target_pairs={{0,8},{1,9},{2,10},{3,11},{4,12},{5,13},{6,14},{7,15},{8,0},{9,1},... | collective-permute-start | bytes 491528 | tf_op jit(solution)/shard_map/ppermute | solution.py:528
  69.0 24.9 %collective-permute-start.3 = (f32[5,64,128]{2,1,0:T(8,128)S(1)}, f32[5,64,128]{2,1,0:T(8,128)S(1)}, u32[]{:S(2)}, u32[]{:S(2)}) collective-permute-start(f32[5,64,128]{2,1,0:T(8,128)S(1)} %shard_map.48), channel_id=1, source_target_pairs={{8,17},{9,18},{10,19},{11,20},{12,21},{13,22},{14,23},{16,9},{17,1... | collective-permute-start | bytes 491528 | tf_op jit(solution)/shard_map/ppermute | solution.py:528
  74.4 11.1 %copy-start.2 = (s32[128]{0:T(128)S(1)}, s32[128]{0:T(128)}, u32[]{:S(2)}) copy-start(s32[128]{0:T(128)} %offsets.9) | copy-start | bytes 1540
  74.4 11.1 %copy-start.3 = (f32[128]{0:T(128)S(1)}, f32[128]{0:T(128)}, u32[]{:S(2)}) copy-start(f32[128]{0:T(128)} %weights.9) | copy-start | bytes 1540
  74.4 19.5 %collective-permute-start.4 = (f32[5,64,128]{2,1,0:T(8,128)S(1)}, f32[5,64,128]{2,1,0:T(8,128)S(1)}, u32[]{:S(2)}, u32[]{:S(2)}) collective-permute-start(f32[5,64,128]{2,1,0:T(8,128)S(1)} %shard_map.49), channel_id=1, source_target_pairs={{0,8},{1,9},{2,10},{3,11},{4,12},{5,13},{6,14},{7,15},{8,0},{9,1},... | collective-permute-start | bytes 491528 | tf_op jit(solution)/shard_map/ppermute | solution.py:528
  99.2 1.6 %copy-start.4 = (s32[16]{0:T(128)S(1)}, s32[16]{0:T(128)}, u32[]{:S(2)}) copy-start(s32[16]{0:T(128)} %counts.3) | copy-start | bytes 196
  100.0 45.7 %collective-permute-start.14 = (f32[4,16,64,128]{3,2,1,0:T(8,128)S(1)}, f32[4,16,64,128]{3,2,1,0:T(8,128)S(1)}, u32[]{:S(2)}, u32[]{:S(2)}) collective-permute-start(f32[4,16,64,128]{3,2,1,0:T(8,128)S(1)} %shard_map.57), channel_id=1, source_target_pairs={{0,8},{1,9},{2,10},{3,11},{4,12},{5,13},{6,14},{7,15},{8,0},{9,1},... | collective-permute-start | bytes 6291464 | tf_op jit(solution)/shard_map/ppermute | solution.py:528
  100.1 0.7 collective-permute-start.6
  101.5 11.2 %collective-permute-start.7 = (f32[2,8,64,128]{3,2,1,0:T(8,128)S(1)}, f32[2,8,64,128]{3,2,1,0:T(8,128)S(1)}, u32[]{:S(2)}, u32[]{:S(2)}) collective-permute-start(f32[2,8,64,128]{3,2,1,0:T(8,128)S(1)} %shard_map.53), channel_id=1, source_target_pairs={{8,16},{9,17},{10,18},{11,19},{12,20},{13,21},{14,22},{15,23},{16,... | collective-permute-start | bytes 1572872 | tf_op jit(solution)/shard_map/ppermute | solution.py:528
  103.4 14.2 %collective-permute-start.8 = (f32[2,8,64,128]{3,2,1,0:T(8,128)S(1)}, f32[2,8,64,128]{3,2,1,0:T(8,128)S(1)}, u32[]{:S(2)}, u32[]{:S(2)}) collective-permute-start(f32[2,8,64,128]{3,2,1,0:T(8,128)S(1)} %get-tuple-element.34), channel_id=1, source_target_pairs={{8,16},{9,17},{10,18},{11,19},{12,20},{13,21},{14,22},{15,23},{16,... | collective-permute-start | bytes 1572872 | tf_op jit(solution)/shard_map/ppermute | solution.py:528
  107.1 33.0 %collective-permute-start.13 = (f32[4,4,64,128]{3,2,1,0:T(8,128)S(1)}, f32[4,4,64,128]{3,2,1,0:T(8,128)S(1)}, u32[]{:S(2)}, u32[]{:S(2)}) collective-permute-start(f32[4,4,64,128]{3,2,1,0:T(8,128)S(1)} %get-tuple-element.37), channel_id=1, source_target_pairs={{8,16},{9,17},{10,18},{11,19},{12,20},{13,21},{14,22},{15,23},{16,... | collective-permute-start | bytes 1572872 | tf_op jit(solution)/shard_map/ppermute | solution.py:528
  109.0 36.7 %collective-permute-start.5 = (f32[4,4,64,128]{3,2,1,0:T(8,128)S(1)}, f32[4,4,64,128]{3,2,1,0:T(8,128)S(1)}, u32[]{:S(2)}, u32[]{:S(2)}) collective-permute-start(f32[4,4,64,128]{3,2,1,0:T(8,128)S(1)} %get-tuple-element.32), channel_id=1, source_target_pairs={{8,16},{9,17},{10,18},{11,19},{12,20},{13,21},{14,22},{15,23},{16,... | collective-permute-start | bytes 1572872 | tf_op jit(solution)/shard_map/ppermute | solution.py:528
  112.7 33.0 %collective-permute-start.9 = (f32[2,8,64,128]{3,2,1,0:T(8,128)S(1)}, f32[2,8,64,128]{3,2,1,0:T(8,128)S(1)}, u32[]{:S(2)}, u32[]{:S(2)}) collective-permute-start(f32[2,8,64,128]{3,2,1,0:T(8,128)S(1)} %collective-permute-done.7.near), channel_id=1, source_target_pairs={{24,33},{25,32},{26,35},{27,34},{28,37},{29,36},{30,39},{31,38},{3... | collective-permute-start | bytes 1572872 | tf_op jit(solution)/shard_map/ppermute | solution.py:528
